TPU v7x, 32 devices: a whole 2x2x4 slice. The times are simulated.
32 devices in a mesh: bank: 8 (over z, y), feat: 4 (over x, core).
Axes of the slice: x: 2, y: 2, z: 4, core: 2. Of those that a mesh axis runs over, the one named last changes fastest.
Arguments:
- bank_rows: bfloat16 [12288, 1536], P('bank', 'feat'), may hold values from -16 to 16
- offsets: int32 [17], replicated, may hold values from 0 to 24576, as said below
Outputs:
- whitened: bfloat16 [12288, 1536], P('bank', 'feat')
Inputs may be any that keep to these rules, and one draw needn't show every extreme that they name: offsets[0] = 0 and offsets[16] = 24576; cluster k holds the rows offsets[k] to offsets[k+1] - 1, and every cluster holds 1152 to 1920 rows, both counts reached in every draw.
All inputs are finite; a program needn't handle non-finite values.
Results may differ from a plain program's by a relative error of at most 0.0058.
Values may be sent and summed in bfloat16 or wider, within the bound.
A program may use at most 128 MiB of HBM per device.

v0:
```python
import jax
import jax.numpy as jnp
from jax import lax
from jax.sharding import PartitionSpec as P

TOUCH = 4


ridge_shift = 0.5


def passed_along(value, axis, steps):
    count = lax.axis_size(axis)
    initial, last = (max(0, -steps), min(count, count - steps))
    return lax.ppermute(value, axis, [(source, source + steps) for source in range(initial, last)])


def transposed_product(left_rows, right_rows):
    return lax.dot_general(
        left_rows, right_rows, (((0,), (0,)), ((), ())), preferred_element_type=jnp.float32
    )


def add_slot(gram_tiles, term, slot_index):
    current = lax.dynamic_index_in_dim(gram_tiles, slot_index, 0, keepdims=False)
    return lax.dynamic_update_index_in_dim(gram_tiles, current + term, slot_index, 0)


def pick_slot(stacked, slot_index):
    return lax.dynamic_index_in_dim(stacked, slot_index, 0, keepdims=False)


def factor_inverse(gram_chosen, offsets, slot_ids, first_label, last_label):
    cluster_count = offsets.shape[0] - 1
    full_width = gram_chosen.shape[1]
    slot_labels = first_label + slot_ids
    in_range = jnp.logical_and(slot_ids < TOUCH, slot_labels <= last_label)
    clamped = jnp.minimum(slot_labels, cluster_count - 1)
    row_counts = (offsets[clamped + 1] - offsets[clamped]).astype(jnp.float32)
    identity = jnp.eye(full_width, dtype=jnp.float32)
    covariance = gram_chosen / row_counts[:, None, None] + ridge_shift * identity
    covariance = jnp.where(in_range[:, None, None], covariance, identity)
    factor = jnp.linalg.cholesky(covariance)
    return lax.linalg.triangular_solve(
        factor, jnp.broadcast_to(identity, covariance.shape), left_side=True, lower=True
    )


def pick_parity(block_part, parity):
    paired = block_part.reshape(block_part.shape[0] // 2, 2, block_part.shape[1])
    return lax.dynamic_index_in_dim(paired, parity, 1, keepdims=False)


def shards(bank_rows, offsets):
    pair_rows, out_width = bank_rows.shape
    rows_dev = pair_rows * 2
    gathered_pairs = lax.all_gather(bank_rows, "feat", axis=1, tiled=True)
    full_width = gathered_pairs.shape[1] // 2
    gathered = gathered_pairs.reshape(rows_dev, full_width)
    row_start = lax.axis_index("bank") * rows_dev
    pair_column = lax.axis_index("feat") * out_width
    parity = pair_column // full_width
    boundaries = offsets[1:-1]
    positions = row_start + jnp.arange(rows_dev, dtype=jnp.int32)
    row_labels = jnp.sum((boundaries[None, :] <= positions[:, None]).astype(jnp.int32), axis=1)
    first_label = row_labels[0]
    last_label = row_labels[rows_dev - 1]
    block_rows = min(512, rows_dev // 4)
    block_total = rows_dev // block_rows

    def split_rows(block_index):
        offset_row = block_index * block_rows
        block_data = lax.dynamic_slice_in_dim(gathered, offset_row, block_rows, 0)
        block_labels = lax.dynamic_slice_in_dim(row_labels, offset_row, block_rows, 0)
        lead_label = block_labels[0]
        later_mask = (block_labels != lead_label).astype(jnp.bfloat16)[:, None]
        later_rows = block_data * later_mask
        early_rows = block_data - later_rows
        return (offset_row, block_data, early_rows, later_rows, lead_label - first_label)

    def accumulate(block_index, gram_tiles):
        offset_row, block_data, early_rows, later_rows, slot_index = split_rows(block_index)
        gram_tiles = add_slot(gram_tiles, transposed_product(early_rows, block_data), slot_index)
        return add_slot(
            gram_tiles,
            transposed_product(later_rows, block_data),
            jnp.minimum(slot_index + 1, TOUCH - 1),
        )

    gram_tiles = lax.fori_loop(
        0, block_total, accumulate, jnp.zeros((TOUCH, full_width, full_width), jnp.float32)
    )
    slot_last = last_label - first_label
    left_open = offsets[first_label] < row_start
    right_open = offsets[last_label + 1] > row_start + rows_dev
    own_first = gram_tiles[0]
    own_last = pick_slot(gram_tiles, slot_last)
    from_right = passed_along(own_first, "bank", -1)
    gram_tiles = add_slot(gram_tiles, jnp.where(right_open, from_right, 0.0), slot_last)
    from_left = passed_along(own_last, "bank", 1)
    gram_tiles = add_slot(gram_tiles, jnp.where(left_open, from_left, 0.0), 0)
    feat_count = lax.axis_size("feat")
    owned_count = (TOUCH + feat_count - 1) // feat_count
    slot_ids = lax.axis_index("feat") + feat_count * jnp.arange(owned_count, dtype=jnp.int32)
    gram_chosen = jnp.take(gram_tiles, jnp.minimum(slot_ids, TOUCH - 1), axis=0)
    inverse = factor_inverse(gram_chosen, offsets, slot_ids, first_label, last_label).astype(
        jnp.bfloat16
    )
    row_pieces = inverse.reshape(owned_count, feat_count // 2, out_width, full_width)
    target_piece = jnp.arange(feat_count, dtype=jnp.int32) % (feat_count // 2)
    outgoing = jnp.swapaxes(jnp.take(row_pieces, target_piece, axis=1), 0, 1)
    incoming = lax.all_to_all(outgoing, "feat", split_axis=0, concat_axis=0, tiled=True)
    factor_rows = jnp.swapaxes(incoming, 0, 1).reshape(
        owned_count * feat_count, out_width, full_width
    )

    def whiten(block_index, whitened):
        offset_row, block_data, early_rows, later_rows, slot_index = split_rows(block_index)
        early_own = pick_parity(early_rows, parity)
        later_own = pick_parity(later_rows, parity)
        first_factor = pick_slot(factor_rows, slot_index)
        second_factor = pick_slot(factor_rows, jnp.minimum(slot_index + 1, TOUCH - 1))
        product_rows = lax.dot_general(
            early_own, first_factor, (((1,), (1,)), ((), ())), preferred_element_type=jnp.float32
        )
        product_rows = product_rows + lax.dot_general(
            later_own, second_factor, (((1,), (1,)), ((), ())), preferred_element_type=jnp.float32
        )
        return lax.dynamic_update_slice_in_dim(
            whitened, product_rows.astype(jnp.bfloat16), offset_row // 2, 0
        )

    return lax.fori_loop(0, block_total, whiten, jnp.zeros((pair_rows, out_width), jnp.bfloat16))


def solution(mesh):
    return jax.shard_map(
        shards,
        mesh=mesh,
        in_specs=(P("bank", "feat"), P()),
        out_specs=P("bank", "feat"),
        check_vma=False,
    )
```

profile of v0, /device:TPU:8, one launch (start us, length us, event | category | flops | bytes accessed | tf_op | source)
XLA Modules:
  0.0 607.8 jit_solution(5781572286215956854)
XLA Ops:
  9.9 37.6 %all-gather.2.cloned.1.call-done = bf16[1536,1536]{1,0:T(8,128)(2,1)} async-done(((bf16[1536,384]{1,0:T(8,128)(2,1)}), bf16[1536,1536]{1,0:T(8,128)(2,1)}) %all-gather.2.cloned.1.call-update) | async-done | bytes 4718608 | tf_op jit(solution)/shard_map/all_gather | solution.py:57
  47.5 8.0 %reshape.458 = bf16[3072,768]{1,0:T(8,128)(2,1)} reshape(bf16[1536,1536]{1,0:T(8,128)(2,1)} %all-gather.2.cloned.1.call-done) | data formatting | bytes 9437184 | tf_op jit(solution)/shard_map/reshape | solution.py:59
  55.5 4.4 broadcast_in_dim.95
  59.9 82.8 %while.32 = (s32[]{:T(128)}, f32[4,768,768]{2,1,0:T(8,128)}, s32[3072]{0:T(1024)S(1)}, s32[]{:T(128)}, bf16[3072,768]{1,0:T(8,128)(2,1)}, /*index=5*/s32[]{:T(12...) while((s32[]{:T(128)}, f32[4,768,768]{2,1,0:T(8,128)}, s32[3072]{0:T(1024)S(1)}, ...), condition=%wide.region_2.3_spmd, body=%wide.region_1.2_spmd.sunk | while | flops 1212679168 | bytes 22032672 | solution.py:90
  97.5 3.8 bitcast_dynamic-update-slice_fusion.8
  142.7 4.1 slice_bitcast_fusion.1
  163.1 89.9 %collective-permute-done = f32[768,768]{1,0:T(8,128)} collective-permute-done((f32[768,768]{1,0:T(8,128)}, f32[768,768]{1,0:T(8,128)}, u32[]{:S(2)}, u32[]{:S(2)}) %collective-permute-start) | collective-permute-done | bytes 2359328 | tf_op jit(solution)/shard_map/ppermute | solution.py:15
  256.4 4.1 fusion.21
  269.2 11.7 %custom-call.52 = f32[1,128,128]{2,1,0:T(8,128)S(1)} custom-call(f32[1,128,128]{2,1,0:T(8,128)S(1)} %cholesky.421), custom_call_target="Cholesky" | custom-call | tf_op jit(solution)/shard_map/jit(cholesky)/cholesky | solution.py:43
  281.1 9.8 %custom-call.53 = f32[1,1,128,128]{2,3,1,0:T(8,128)S(1)} custom-call(f32[1,1,128,128]{3,2,1,0:T(8,128)S(1)} %get-tuple-element.378), custom_call_target="InvertDiagBlocksLowerTriangular" | custom-call | tf_op jit(solution)/shard_map/jit(cholesky)/cholesky | solution.py:43
  293.7 11.7 %custom-call.54 = f32[1,128,128]{2,1,0:T(8,128)S(1)} custom-call(f32[1,128,128]{2,1,0:T(8,128)S(1)} %cholesky.425), custom_call_target="Cholesky" | custom-call | tf_op jit(solution)/shard_map/jit(cholesky)/cholesky | solution.py:43
  305.5 10.0 %custom-call.55 = f32[1,1,128,128]{2,3,1,0:T(8,128)S(1)} custom-call(f32[1,1,128,128]{3,2,1,0:T(8,128)S(1)} %get-tuple-element.375), custom_call_target="InvertDiagBlocksLowerTriangular" | custom-call | tf_op jit(solution)/shard_map/jit(cholesky)/cholesky | solution.py:43
  317.3 11.7 %custom-call.56 = f32[1,128,128]{2,1,0:T(8,128)S(1)} custom-call(f32[1,128,128]{2,1,0:T(8,128)S(1)} %cholesky.430), custom_call_target="Cholesky" | custom-call | tf_op jit(solution)/shard_map/jit(cholesky)/cholesky | solution.py:43
  329.7 9.8 %custom-call.57 = f32[1,1,128,128]{2,3,1,0:T(8,128)S(1)} custom-call(f32[1,1,128,128]{3,2,1,0:T(8,128)S(1)} %get-tuple-element.372), custom_call_target="InvertDiagBlocksLowerTriangular" | custom-call | tf_op jit(solution)/shard_map/jit(cholesky)/cholesky | solution.py:43
  341.4 12.1 %custom-call.58 = f32[1,128,128]{2,1,0:T(8,128)S(1)} custom-call(f32[1,128,128]{2,1,0:T(8,128)S(1)} %cholesky.435), custom_call_target="Cholesky" | custom-call | tf_op jit(solution)/shard_map/jit(cholesky)/cholesky | solution.py:43
  354.2 9.8 %custom-call.59 = f32[1,1,128,128]{2,3,1,0:T(8,128)S(1)} custom-call(f32[1,1,128,128]{3,2,1,0:T(8,128)S(1)} %get-tuple-element.369), custom_call_target="InvertDiagBlocksLowerTriangular" | custom-call | tf_op jit(solution)/shard_map/jit(cholesky)/cholesky | solution.py:43
  365.8 11.7 %custom-call.60 = f32[1,128,128]{2,1,0:T(8,128)S(1)} custom-call(f32[1,128,128]{2,1,0:T(8,128)S(1)} %cholesky.440), custom_call_target="Cholesky" | custom-call | tf_op jit(solution)/shard_map/jit(cholesky)/cholesky | solution.py:43
  378.3 9.8 %custom-call.61 = f32[1,1,128,128]{2,3,1,0:T(8,128)S(1)} custom-call(f32[1,1,128,128]{3,2,1,0:T(8,128)S(1)} %get-tuple-element.366), custom_call_target="InvertDiagBlocksLowerTriangular" | custom-call | tf_op jit(solution)/shard_map/jit(cholesky)/cholesky | solution.py:43
  389.6 11.9 %custom-call.62 = f32[1,128,128]{2,1,0:T(8,128)S(1)} custom-call(f32[1,128,128]{2,1,0:T(8,128)S(1)} %slice_subtract_fusion.4), custom_call_target="Cholesky" | custom-call | tf_op jit(solution)/shard_map/jit(cholesky)/cholesky | solution.py:43
  408.3 16.7 %while.34 = (s32[]{:T(128)}, f32[1,768,768]{2,1,0:T(8,128)}, s32[6,2]{0,1:T(2,128)S(1)}, f32[6,1,128,128]{3,2,1,0:T(8,128)S(1)}, s32[]{:T(128)}) while((s32[]{:T(128)}, f32[1,768,768]{2,1,0:T(8,128)}, s32[6,2]{0,1:T(2,128)S(1)}, f32[6,1,128,128]{3,2,1,0:T(8,128)S(1)}, s32[]{:T(128)}) %tuple.119), condition=%wide.while_cond.3, body=%wide.while_body.3.sunk | while | flops 2 | bytes 131181 | solution.py:44
  425.0 59.6 %custom-call.63 = f32[1,6,128,128]{2,3,1,0:T(8,128)} custom-call(f32[1,6,128,128]{3,2,1,0:T(8,128)S(1)} %bitcast.351), custom_call_target="InvertDiagBlocksLowerTriangular" | custom-call | tf_op jit(solution)/shard_map/triangular_solve | solution.py:44
  500.8 4.5 all-to-all-start
  505.3 28.5 %all-to-all-done = bf16[4,1,384,768]{3,2,1,0:T(8,128)(2,1)} async-done(((bf16[4,1,384,768]{3,2,1,0:T(8,128)(2,1)}), bf16[4,1,384,768]{3,2,1,0:T(8,128)(2,1)}, u32[]{:S(2)}, u32[]{:S(2)}) %all-to-all-start) | async-done | bytes 2359328 | tf_op jit(solution)/shard_map/all_to_all | solution.py:112
  535.0 65.8 %while.33 = (s32[]{:T(128)}, bf16[1536,384]{1,0:T(8,128)(2,1)}, bf16[3072,768]{1,0:T(8,128)(2,1)}, s32[3072]{0:T(1024)S(1)}, s32[]{:T(128)}, /*index=5*/s32[]{:T...) while((s32[]{:T(128)}, bf16[1536,384]{1,0:T(8,128)(2,1)}, ...), condition=%wide.region_16.17_spmd, body=%wide.region_15.16_spmd.sunk | while | flops 304546816 | bytes 10428922 | solution.py:133
  (196 shorter events, 202.8 us)
Async XLA Ops:
  6.5 41.0 %all-gather.2.cloned.1.call-start = ((), (), s32[]{:S(2)}) async-start(), calls=%async_computation.1 | async-start | bytes 5898240 | tf_op jit(solution)/shard_map/all_gather | solution.py:57
  142.7 14.2 %copy-start.3 = (s32[17]{0:T(128)S(1)}, s32[17]{0:T(128)}, u32[]{:S(2)}) copy-start(s32[17]{0:T(128)} %param.7) | copy-start | bytes 208
  146.9 106.2 %collective-permute-start = (f32[768,768]{1,0:T(8,128)}, f32[768,768]{1,0:T(8,128)}, u32[]{:S(2)}, u32[]{:S(2)}) collective-permute-start(f32[768,768]{1,0:T(8,128)} %get-tuple-element.361), channel_id=1, source_target_pairs={{4,0},{8,4},{12,8},{16,12},{20,16},{24,20},{28,24},{5,1},{9,5},{13... | collective-permute-start | bytes 7077896 | tf_op jit(solution)/shard_map/ppermute | solution.py:15
  150.2 106.2 %collective-permute-start.1 = (f32[768,768]{1,0:T(8,128)S(1)}, f32[768,768]{1,0:T(8,128)}, u32[]{:S(2)}, u32[]{:S(2)}) collective-permute-start(f32[768,768]{1,0:T(8,128)S(1)} %get-tuple-element.362), channel_id=1, source_target_pairs={{0,4},{4,8},{8,12},{12,16},{16,20},{20,24},{24,28},{1,5},{5,9},{9,... | collective-permute-start | bytes 7077896 | tf_op jit(solution)/shard_map/ppermute | solution.py:15
  267.8 1.4 copy-start.1
  425.0 63.0 %copy-start = (f32[1,768,768]{2,1,0:T(8,128)S(1)}, f32[1,768,768]{2,1,0:T(8,128)}, u32[]{:S(2)}) copy-start(f32[1,768,768]{2,1,0:T(8,128)} %fusion.35) | copy-start | bytes 7077892
  484.6 2.8 copy-start.2
  500.8 33.1 %all-to-all-start = ((bf16[4,1,384,768]{3,2,1,0:T(8,128)(2,1)}), bf16[4,1,384,768]{3,2,1,0:T(8,128)(2,1)}, u32[]{:S(2)}, u32[]{:S(2)}) async-start(bf16[4,1,384,768]{3,2,1,0:T(8,128)(2,1)} %bitcast_select_fusion), calls=%async_computation | async-start | bytes 4718592 | tf_op jit(solution)/shard_map/all_to_all | solution.py:112
Sparse Core Ops, SparseCore 0:
  8.9 38.5 all-gather.1
where the time goes:
time: 616 us; the launch traced here: 608 us
  other arithmetic  220 us (36%)
  waiting for transfers between devices  157 us (25%)
  local copies, waits for them, and re-layouts  95.8 us (16%)
  matrix products  84.9 us (14%)
  between operations  25.6 us (4%)
  loops' own time  15 us (2%)
  starting transfers between devices  10.3 us (2%)
    another operation x22, other arithmetic, factor_inverse(): factor = jnp.linalg.cholesky(covariance)  124 us
    ppermute x2, waiting for transfers between devices, passed_along(): lax.ppermute(value, axis, [(source, source + steps) for source in range(i...  89.9 us
    another operation x3, other arithmetic, factor_inverse(): lax.linalg.triangular_solve(factor, jnp.broadcast_to(identity, covariance...  61.2 us
    dot_general x12, matrix products, transposed_product(): lax.dot_general(left_rows, right_rows, (((0,), (0,)), ((), ())), preferre...  44.8 us
    all_gather x1, waiting for transfers between devices, shards(): gathered_pairs = lax.all_gather(bank_rows, 'feat', axis=1, tiled=True)  37.6 us
    all_to_all x1, waiting for transfers between devices, shards(): lax.all_to_all(outgoing, 'feat', split_axis=0, concat_axis=0, tiled=True)  28.5 us
    dynamic_slice x12, local copies, waits for them, and re-layouts, add_slot(): lax.dynamic_index_in_dim(gram_tiles, slot_index, 0, keepdims=False)  21.8 us
    another operation x18, local copies, waits for them, and re-layouts  16.6 us
  transfers between devices with their start and end apart: 4, of which 3 were waited for; matrix products, arithmetic and copies ran while one was open for 1% of the time, Pallas kernels for 0%

commit v1 on v0

v1 whole, which is shorter than its diff:
```python
import jax
import jax.numpy as jnp
from jax import lax
from jax.experimental import pallas as pl
from jax.experimental.pallas import tpu as pltpu
from jax.sharding import PartitionSpec as P

TOUCH = 4
BLOCK = 128
SUB = 8
ridge_shift = 0.5


def slot_bounds(offsets, row_start, rows_dev):
    boundaries = offsets[1:-1]
    first_label = jnp.sum((boundaries <= row_start).astype(jnp.int32))
    last_label = jnp.sum((boundaries <= row_start + rows_dev - 1).astype(jnp.int32))
    roles = jnp.arange(TOUCH, dtype=jnp.int32)
    labels = jnp.where(
        roles == TOUCH - 1, last_label, jnp.minimum(first_label + roles, last_label)
    )
    used = jnp.logical_or(roles == TOUCH - 1, first_label + roles < last_label)
    low = jnp.clip(offsets[labels] - row_start, 0, rows_dev)
    high = jnp.clip(offsets[labels + 1] - row_start, 0, rows_dev)
    high = jnp.where(used, high, low)
    counts = offsets[labels + 1] - offsets[labels]
    return low, high, counts, first_label, last_label


def gram_kernel(bounds, pairs_ref, gram_ref):
    step = pl.program_id(0)
    block_pairs = pairs_ref.shape[0]
    width = pairs_ref.shape[1] // 2
    low, high = bounds[0], bounds[1]
    start = step * block_pairs * 2

    @pl.when(step == 0)
    def _():
        gram_ref[...] = jnp.zeros_like(gram_ref)

    @pl.when(jnp.logical_and(start < high, start + 2 * block_pairs > low))
    def _():
        row = start + 2 * lax.broadcasted_iota(jnp.int32, (block_pairs, 1), 0)
        for parity in range(2):
            data = pairs_ref[:, parity * width : (parity + 1) * width]
            keep = jnp.logical_and(row + parity >= low, row + parity < high)
            data = jnp.where(keep, data, jnp.zeros_like(data))
            gram_ref[...] += lax.dot_general(
                data, data, (((0,), (0,)), ((), ())), preferred_element_type=jnp.float32
            )


def own_gram(pairs, bounds):
    pair_rows, pair_width = pairs.shape
    width = pair_width // 2
    block_pairs = min(256, pair_rows)
    return pl.pallas_call(
        gram_kernel,
        grid_spec=pltpu.PrefetchScalarGridSpec(
            num_scalar_prefetch=1,
            grid=(pair_rows // block_pairs,),
            in_specs=[pl.BlockSpec((block_pairs, pair_width), lambda i, b: (i, 0))],
            out_specs=pl.BlockSpec((width, width), lambda i, b: (0, 0)),
        ),
        out_shape=jax.ShapeDtypeStruct((width, width), jnp.float32),
        compiler_params=pltpu.CompilerParams(vmem_limit_bytes=32 << 20),
    )(bounds, pairs)


def split_rows(value):
    high = value.astype(jnp.bfloat16).astype(jnp.float32)
    rest = value - high
    middle = rest.astype(jnp.bfloat16).astype(jnp.float32)
    low = (rest - middle).astype(jnp.bfloat16).astype(jnp.float32)
    return high, middle, low


def factor_block(work):
    for panel in range(BLOCK // SUB):
        base = panel * SUB
        rows = [work[base + i : base + i + 1, :] for i in range(SUB)]
        entry = {}
        for i in range(SUB):
            for k in range(i, SUB):
                column = base + k
                entry[i, k] = jnp.broadcast_to(rows[i][:, column : column + 1], (1, BLOCK))
        done = []
        for i in range(SUB):
            inverse_root = lax.rsqrt(entry[i, i])
            coefficient = {k: entry[i, k] * inverse_root for k in range(i + 1, SUB)}
            for k in range(i + 1, SUB):
                for m in range(k, SUB):
                    entry[k, m] = entry[k, m] - coefficient[k] * coefficient[m]
            scaled = rows[i] * jnp.concatenate([inverse_root, inverse_root], axis=1)
            done.append(scaled)
            for k in range(i + 1, SUB):
                both = jnp.concatenate([coefficient[k], coefficient[k]], axis=1)
                rows[k] = rows[k] - both * scaled
        for i in range(SUB):
            work[base + i : base + i + 1, :] = done[i]
        if base + SUB < BLOCK:
            high, middle, low = split_rows(work[base : base + SUB, :])
            left = jnp.concatenate([high, high, middle, high, middle, low], axis=0)
            right = jnp.concatenate([high, middle, high, low, middle, high], axis=0)
            update = lax.dot_general(
                left[:, :BLOCK].astype(jnp.bfloat16),
                right.astype(jnp.bfloat16),
                (((0,), (0,)), ((), ())),
                preferred_element_type=jnp.float32,
            )
            work[base + SUB :, :] = work[base + SUB :, :] - update[base + SUB :, :]


def whitener_kernel(scalars, own_ref, other_ref, out_ref, matrix, work):
    width = own_ref.shape[0]
    blocks = width // BLOCK
    joined = scalars[0] > 0
    count = scalars[1].astype(jnp.float32)
    eye = (
        lax.broadcasted_iota(jnp.int32, (BLOCK, BLOCK), 0)
        == lax.broadcasted_iota(jnp.int32, (BLOCK, BLOCK), 1)
    ).astype(jnp.float32)
    for i in range(blocks):
        span = slice(i * BLOCK, (i + 1) * BLOCK)
        total = own_ref[span, :] + jnp.where(joined, other_ref[span, :], 0.0)
        matrix[span, :width] = total / count
        matrix[span, width:] = jnp.zeros((BLOCK, width), jnp.float32)
    for i in range(blocks):
        span = slice(i * BLOCK, (i + 1) * BLOCK)
        matrix[span, span] = matrix[span, span] + ridge_shift * eye
        matrix[span, width + i * BLOCK : width + (i + 1) * BLOCK] = eye

    @pl.loop(0, blocks)
    def _(j):
        here = pl.multiple_of(j * BLOCK, BLOCK)
        work[:, :BLOCK] = matrix[pl.ds(here, BLOCK), pl.ds(here, BLOCK)]
        work[:, BLOCK:] = eye
        factor_block(work)
        panel = lax.dot_general(
            work[:, BLOCK:],
            matrix[pl.ds(here, BLOCK), :],
            (((1,), (0,)), ((), ())),
            precision=lax.Precision.HIGHEST,
            preferred_element_type=jnp.float32,
        )
        matrix[pl.ds(here, BLOCK), :] = panel

        @pl.loop(j + 1, blocks)
        def _(i):
            there = pl.multiple_of(i * BLOCK, BLOCK)
            update = lax.dot_general(
                matrix[pl.ds(here, BLOCK), pl.ds(there, BLOCK)],
                matrix[pl.ds(here, BLOCK), :],
                (((0,), (0,)), ((), ())),
                precision=lax.Precision.HIGHEST,
                preferred_element_type=jnp.float32,
            )
            matrix[pl.ds(there, BLOCK), :] = matrix[pl.ds(there, BLOCK), :] - update

    out_ref[...] = matrix[:, width:].astype(jnp.bfloat16)


def own_whitener(scalars, own, other):
    width = own.shape[0]
    return pl.pallas_call(
        whitener_kernel,
        in_specs=[
            pl.BlockSpec(memory_space=pltpu.SMEM),
            pl.BlockSpec(memory_space=pltpu.VMEM),
            pl.BlockSpec(memory_space=pltpu.VMEM),
        ],
        out_specs=pl.BlockSpec(memory_space=pltpu.VMEM),
        out_shape=jax.ShapeDtypeStruct((width, width), jnp.bfloat16),
        scratch_shapes=[
            pltpu.VMEM((width, 2 * width), jnp.float32),
            pltpu.VMEM((BLOCK, 2 * BLOCK), jnp.float32),
        ],
        compiler_params=pltpu.CompilerParams(vmem_limit_bytes=40 << 20),
    )(scalars, own, other)


def whiten_kernel(scalars, rows_ref, factor_ref, out_ref, total):
    step = pl.program_id(0)
    block_pairs = rows_ref.shape[0]
    parity = scalars[0]
    start = step * block_pairs * 2
    row = start + parity + 2 * lax.broadcasted_iota(jnp.int32, (block_pairs, 1), 0)
    total[...] = jnp.zeros_like(total)
    for role in range(TOUCH):
        low, high, place = scalars[1 + role], scalars[1 + TOUCH + role], scalars[1 + 2 * TOUCH + role]

        @pl.when(jnp.logical_and(start < high, start + 2 * block_pairs > low))
        def _():
            data = rows_ref[...]
            keep = jnp.logical_and(row >= low, row < high)
            data = jnp.where(keep, data, jnp.zeros_like(data))
            total[...] += lax.dot_general(
                data, factor_ref[place], (((1,), (1,)), ((), ())), preferred_element_type=jnp.float32
            )

    out_ref[...] = total[...].astype(jnp.bfloat16)


def whiten(scalars, pairs, factor_rows):
    pair_rows, pair_width = pairs.shape
    width = pair_width // 2
    out_width = factor_rows.shape[1]
    block_pairs = min(256, pair_rows)
    return pl.pallas_call(
        whiten_kernel,
        grid_spec=pltpu.PrefetchScalarGridSpec(
            num_scalar_prefetch=1,
            grid=(pair_rows // block_pairs,),
            in_specs=[
                pl.BlockSpec((block_pairs, width), lambda i, s: (i, s[0])),
                pl.BlockSpec(factor_rows.shape, lambda i, s: (0, 0, 0)),
            ],
            out_specs=pl.BlockSpec((block_pairs, out_width), lambda i, s: (i, 0)),
            scratch_shapes=[pltpu.VMEM((block_pairs, out_width), jnp.float32)],
        ),
        out_shape=jax.ShapeDtypeStruct((pair_rows, out_width), jnp.bfloat16),
        compiler_params=pltpu.CompilerParams(vmem_limit_bytes=32 << 20),
    )(scalars, pairs, factor_rows)


def meeting_pairs(bank_count, feat_count):
    pairs = []
    for bank in range(bank_count - 1):
        place = feat_count - 1 if bank % 2 == 0 else 0
        left, right = bank * feat_count + place, (bank + 1) * feat_count + place
        pairs += [(left, right), (right, left)]
    return pairs


def shards(bank_rows, offsets):
    pair_rows, out_width = bank_rows.shape
    rows_dev = pair_rows * 2
    bank, feat = lax.axis_index("bank"), lax.axis_index("feat")
    bank_count, feat_count = lax.axis_size("bank"), lax.axis_size("feat")
    pairs = lax.all_gather(bank_rows, "feat", axis=1, tiled=True)
    full_width = pairs.shape[1] // 2
    row_start = bank * rows_dev
    low, high, counts, first_label, last_label = slot_bounds(offsets, row_start, rows_dev)
    roles = jnp.arange(TOUCH, dtype=jnp.int32)
    places = jnp.where(bank % 2 == 0, roles, TOUCH - 1 - roles)
    role = jnp.where(bank % 2 == 0, feat, TOUCH - 1 - feat)
    own = own_gram(pairs, jnp.stack([low[role], high[role]]))
    other = lax.ppermute(own, ("bank", "feat"), meeting_pairs(bank_count, feat_count))
    left_open = offsets[first_label] < row_start
    right_open = offsets[last_label + 1] > row_start + rows_dev
    joined = jnp.logical_or(
        jnp.logical_and(role == 0, left_open), jnp.logical_and(role == TOUCH - 1, right_open)
    )
    inverse = own_whitener(jnp.stack([joined.astype(jnp.int32), counts[role]]), own, other)
    halves = inverse.reshape(feat_count // 2, out_width, full_width)
    outgoing = jnp.concatenate([halves] * 2, axis=0)
    factor_rows = lax.all_to_all(outgoing, "feat", split_axis=0, concat_axis=0, tiled=True)
    parity = feat * out_width // full_width
    scalars = jnp.concatenate([parity[None].astype(jnp.int32), low, high, places])
    return whiten(scalars, pairs, factor_rows)


def solution(mesh):
    return jax.shard_map(
        shards,
        mesh=mesh,
        in_specs=(P("bank", "feat"), P()),
        out_specs=P("bank", "feat"),
        check_vma=False,
    )
```

time: 616 us -> 187 us (0.30); the launches traced: 608 us -> 185 us
  other arithmetic: 220 us -> 7.67 us
  local copies, waits for them, and re-layouts: 95.8 us -> 9.76 us
  matrix products: 84.9 us -> 0 us
  waiting for transfers between devices: 157 us -> 81.1 us
  Pallas kernels: 0 us -> 59.3 us
  loops' own time: 15 us -> 0 us
  between operations: 25.6 us -> 17.7 us
    another operation x25 -> x2, other arithmetic: 185 us -> 2.16 us  [the longest x1 1.44 us: shards(): own = own_gram(pairs, jnp.stack([low[role], high[role]]))]
    ppermute x2 -> x1, waiting for transfers between devices: 89.9 us -> 20.8 us  [shards(): lax.ppermute(own, ('bank', 'feat'), meeting_pairs(bank_count, feat_count))]
    dot_general x24 -> x0, matrix products: 62.2 us -> none  [the longest x12 44.8 us: transposed_product(): lax.dot_general(left_rows, right_rows, (((0,), (0,)), ((), ())), preferre...]
    pallas_call x0 -> x3, Pallas kernels: none -> 59.3 us  [the longest x1 51.9 us: own_whitener(): pl.pallas_call(whitener_kernel, in_specs=[pl.BlockSpec(memory_space=pltpu...]
    dynamic_slice x30 -> x4, local copies, waits for them, and re-layouts: 32.5 us -> 2.5 us  [the longest x2 1.32 us: shards(): own = own_gram(pairs, jnp.stack([low[role], high[role]]))]
    another operation x21 -> x0, matrix products: 22.7 us -> none  [the longest x11 12.9 us: factor_inverse(): lax.linalg.triangular_solve(factor, jnp.broadcast_to(identity, covariance...]
    another operation x26 -> x0, local copies, waits for them, and re-layouts: 16.8 us -> none
    another operation x3 -> x0, loops' own time: 15 us -> none  [the longest x1 7.61 us: shards(): lax.fori_loop(0, block_total, accumulate, jnp.zeros((TOUCH, full_width, f...]
  transfers between devices with their start and end apart: 4 -> 3, of which waited for: 3 -> 3; matrix products, arithmetic and copies ran while one was open for 1% -> 6% of each run, Pallas kernels for 0% -> 0%
where the time goes in v1:
time: 187 us; the launch traced here: 185 us
  waiting for transfers between devices  81.1 us (43%)
  Pallas kernels  59.3 us (32%)
  between operations  17.7 us (9%)
  local copies, waits for them, and re-layouts  9.76 us (5%)
  starting transfers between devices  9.53 us (5%)
  other arithmetic  7.67 us (4%)
    pallas_call x1, Pallas kernels, own_whitener(): pl.pallas_call(whitener_kernel, in_specs=[pl.BlockSpec(memory_space=pltpu...  51.9 us
    all_gather x1, waiting for transfers between devices, shards(): pairs = lax.all_gather(bank_rows, 'feat', axis=1, tiled=True)  31.2 us
    all_to_all x1, waiting for transfers between devices, shards(): lax.all_to_all(outgoing, 'feat', split_axis=0, concat_axis=0, tiled=True)  28.4 us
    ppermute x1, waiting for transfers between devices, shards(): lax.ppermute(own, ('bank', 'feat'), meeting_pairs(bank_count, feat_count))  20.8 us
    ppermute x1, starting transfers between devices, shards(): lax.ppermute(own, ('bank', 'feat'), meeting_pairs(bank_count, feat_count))  5.89 us
    pallas_call x1, Pallas kernels, whiten(): pl.pallas_call(whiten_kernel, grid_spec=pltpu.PrefetchScalarGridSpec(num_...  5.76 us
    unnamed x6, local copies, waits for them, and re-layouts  4.68 us
  transfers between devices with their start and end apart: 3, of which 3 were waited for; matrix products, arithmetic and copies ran while one was open for 6% of the time, Pallas kernels for 0%

profile of v1, /device:TPU:8, one launch (start us, length us, event | category | flops | bytes accessed | tf_op | source)
XLA Modules:
  0.0 185.0 jit_solution(15555275806029202109)
XLA Ops:
  6.5 0.7 all-gather.2.cloned.1.call-update
  7.3 1.4 fusion
  8.6 1.2 fusion.2
  9.9 1.3 gather_fusion
  11.2 1.3 gather_fusion.1
  12.5 1.2 fusion.4
  13.7 0.7 dynamic_slice.18
  14.3 0.7 dynamic_slice.19
  15.0 1.4 pad_add_fusion.2.bounds
  16.4 31.2 %all-gather.2.cloned.1.call-done.pairs_ref.rows_ref = bf16[1536,1536]{1,0:T(8,128)(2,1)} async-done(((bf16[1536,384]{1,0:T(8,128)(2,1)}), bf16[1536,1536]{1,0:T(8,128)(2,1)}) %all-gather.2.cloned.1.call-update) | async-done | bytes 4718608 | tf_op jit(solution)/shard_map/all_gather | solution.py:240
  47.6 2.3 %copy-done = bf16[1536,1536]{1,0:T(8,128)(2,1)S(1)} copy-done((bf16[1536,1536]{1,0:T(8,128)(2,1)S(1)}, bf16[1536,1536]{1,0:T(8,128)(2,1)}, u32[]{:S(2)}) %copy-start) | copy-done | bytes 4718616
  49.9 1.7 shard_map.28.own_ref
  51.6 5.9 %collective-permute-start = (f32[768,768]{1,0:T(8,128)S(1)}, f32[768,768]{1,0:T(8,128)}, u32[]{:S(2)}, u32[]{:S(2)}) collective-permute-start(f32[768,768]{1,0:T(8,128)S(1)} %shard_map.28.own_ref), channel_id=1, source_target_pairs={{3,7},{7,3},{4,8},{8,4},{11,15},{15,11},{12,16},{16,12},{19,23},{2... | collective-permute-start | bytes 7077896 | tf_op jit(solution)/shard_map/ppermute | solution.py:248
  60.5 0.6 fusion.5
  62.3 0.6 dynamic_slice.17
  62.9 0.7 pad_add_fusion.1.scalars
  63.6 20.8 %collective-permute-done.other_ref = f32[768,768]{1,0:T(8,128)} collective-permute-done((f32[768,768]{1,0:T(8,128)S(1)}, f32[768,768]{1,0:T(8,128)}, u32[]{:S(2)}, u32[]{:S(2)}) %collective-permute-start) | collective-permute-done | bytes 2359328 | tf_op jit(solution)/shard_map/ppermute | solution.py:248
  84.4 51.9 %shard_map.29 = bf16[768,768]{1,0:T(8,128)(2,1)S(1)} custom-call(s32[2]{0:T(128)S(1)} %pad_add_fusion.1.scalars, f32[768,768]{1,0:T(8,128)S(1)} %shard_map.28.own_ref, f32[768,768]{1,0:T(8,128)} %collective-permute-done.other_ref), custom_call_target="tpu_custom_call" | custom-call | tf_op jit(solution)/shard_map/pallas_call | solution.py:165
  136.3 1.6 pad_maximum_fusion
  138.0 3.6 %all-to-all-start = ((bf16[4,384,768]{2,1,0:T(8,128)(2,1)}), bf16[4,384,768]{2,1,0:T(8,128)(2,1)S(1)}, u32[]{:S(2)}, u32[]{:S(2)}) async-start(bf16[4,384,768]{2,1,0:T(8,128)(2,1)} %pad_maximum_fusion), calls=%async_computation | async-start | bytes 4718592 | tf_op jit(solution)/shard_map/all_to_all | solution.py:257
  141.7 0.1 pad_add_fusion.scalars
  141.7 28.4 %all-to-all-done.factor_ref = bf16[4,384,768]{2,1,0:T(8,128)(2,1)S(1)} async-done(((bf16[4,384,768]{2,1,0:T(8,128)(2,1)}), bf16[4,384,768]{2,1,0:T(8,128)(2,1)S(1)}, u32[]{:S(2)}, u32[]{:S(2)}) %all-to-all-start) | async-done | bytes 2359328 | tf_op jit(solution)/shard_map/all_to_all | solution.py:257
  170.1 2.3 %copy-done.1 = bf16[1536,1536]{1,0:T(8,128)(2,1)S(1)} copy-done((bf16[1536,1536]{1,0:T(8,128)(2,1)S(1)}, bf16[1536,1536]{1,0:T(8,128)(2,1)}, u32[]{:S(2)}) %copy-start.1) | copy-done | bytes 4718616
  172.4 5.8 %shard_map.30 = bf16[1536,384]{1,0:T(8,128)(2,1)} custom-call(s32[13]{0:T(128)S(1)} %pad_add_fusion.scalars, bf16[1536,1536]{1,0:T(8,128)(2,1)S(1)} %copy-done.1, bf16[4,384,768]{2,1,0:T(8,128)(2,1)S(1)} %all-to-all-done.factor_ref), custom_call_target="tpu_custom_call" | custom-call | tf_op jit(solution)/shard_map/pallas_call | solution.py:209
  (8 shorter events, 0.0 us)
Async XLA Ops:
  6.5 41.1 %all-gather.2.cloned.1.call-start = ((), (), s32[]{:S(2)}) async-start(), calls=%async_computation.1 | async-start | bytes 5898240 | tf_op jit(solution)/shard_map/all_gather | solution.py:240
  47.6 2.3 %copy-start = (bf16[1536,1536]{1,0:T(8,128)(2,1)S(1)}, bf16[1536,1536]{1,0:T(8,128)(2,1)}, u32[]{:S(2)}) copy-start(bf16[1536,1536]{1,0:T(8,128)(2,1)} %all-gather.2.cloned.1.call-done.pairs_ref.rows_ref) | copy-start | bytes 14155780
  49.9 10.5 %copy-start.2 = (s32[17]{0:T(128)S(1)}, s32[17]{0:T(128)}, u32[]{:S(2)}) copy-start(s32[17]{0:T(128)} %param.3) | copy-start | bytes 208
  51.6 32.8 %collective-permute-start = (f32[768,768]{1,0:T(8,128)S(1)}, f32[768,768]{1,0:T(8,128)}, u32[]{:S(2)}, u32[]{:S(2)}) collective-permute-start(f32[768,768]{1,0:T(8,128)S(1)} %shard_map.28.own_ref), channel_id=1, source_target_pairs={{3,7},{7,3},{4,8},{8,4},{11,15},{15,11},{12,16},{16,12},{19,23},{2... | collective-permute-start | bytes 7077896 | tf_op jit(solution)/shard_map/ppermute | solution.py:248
  138.0 32.1 %all-to-all-start = ((bf16[4,384,768]{2,1,0:T(8,128)(2,1)}), bf16[4,384,768]{2,1,0:T(8,128)(2,1)S(1)}, u32[]{:S(2)}, u32[]{:S(2)}) async-start(bf16[4,384,768]{2,1,0:T(8,128)(2,1)} %pad_maximum_fusion), calls=%async_computation | async-start | bytes 4718592 | tf_op jit(solution)/shard_map/all_to_all | solution.py:257
  170.1 2.3 %copy-start.1 = (bf16[1536,1536]{1,0:T(8,128)(2,1)S(1)}, bf16[1536,1536]{1,0:T(8,128)(2,1)}, u32[]{:S(2)}) copy-start(bf16[1536,1536]{1,0:T(8,128)(2,1)} %all-gather.2.cloned.1.call-done.pairs_ref.rows_ref) | copy-start | bytes 14155780
Sparse Core Ops, SparseCore 0:
  8.9 38.6 all-gather.1

commit v2 on v1

v2 whole, which is shorter than its diff:
```python
import functools

import jax
import jax.numpy as jnp
from jax import lax
from jax.experimental import pallas as pl
from jax.experimental.pallas import tpu as pltpu
from jax.sharding import PartitionSpec as P

TOUCH = 4
BLOCK = 128
SUB = 8
ridge_shift = 0.5


MESH = pl.DeviceIdType.MESH
GATHER_CHUNKS = 4


def slot_of(offsets, role, row_start, rows_dev):
    clusters = offsets.shape[0] - 1

    def count(k, found):
        bound = offsets[k]
        first, last = found
        first = first + (bound <= row_start).astype(jnp.int32)
        last = last + (bound <= row_start + rows_dev - 1).astype(jnp.int32)
        return first, last

    first, last = lax.fori_loop(1, clusters, count, (jnp.int32(0), jnp.int32(0)))
    is_last = role == TOUCH - 1
    label = jnp.where(is_last, last, jnp.minimum(first + role, last))
    used = jnp.logical_or(is_last, first + role < last)
    low = jnp.clip(offsets[label] - row_start, 0, rows_dev)
    high = jnp.clip(offsets[label + 1] - row_start, 0, rows_dev)
    return low, jnp.where(used, high, low), label


def own_role():
    feat = lax.axis_index("feat")
    return jnp.where(lax.axis_index("bank") % 2 == 0, feat, TOUCH - 1 - feat)


def neighbours():
    bank, feat = lax.axis_index("bank"), lax.axis_index("feat")
    sibling = feat + 1 - 2 * (feat % 2)
    return bank, sibling, (feat + 2) % TOUCH, (sibling + 2) % TOUCH


def greet(bank, others):
    barrier = pltpu.get_barrier_semaphore()
    for other in others:
        pl.semaphore_signal(barrier, inc=1, device_id=(bank, other), device_id_type=MESH)
    pl.semaphore_wait(barrier, len(others))


def gather_kernel(own, near, across, far, send, receive):
    bank, sibling, partner, _ = neighbours()
    greet(bank, (sibling, partner))
    piece = own.shape[0] // GATHER_CHUNKS

    def remote(source, target, place, device):
        return pltpu.make_async_remote_copy(
            src_ref=source,
            dst_ref=target,
            send_sem=send.at[place],
            recv_sem=receive.at[place],
            device_id=(bank, device),
            device_id_type=MESH,
        )

    firsts, seconds = [], []
    for i in range(GATHER_CHUNKS):
        span = pl.ds(i * piece, piece)
        firsts.append(remote(own.at[span, :], across.at[span, :], i, partner))
        seconds.append(
            remote(across.at[span, :], far.at[span, :], GATHER_CHUNKS + i, sibling)
        )
    beside = remote(own, near, 2 * GATHER_CHUNKS, sibling)
    for copy in firsts:
        copy.start()
    beside.start()
    for first, second in zip(firsts, seconds):
        first.wait_recv()
        second.start()
    for copy in firsts:
        copy.wait_send()
    for copy in seconds:
        copy.wait()
    beside.wait()


def gather_rows(own):
    anywhere = pl.BlockSpec(memory_space=pl.ANY)
    return pl.pallas_call(
        gather_kernel,
        in_specs=[anywhere],
        out_specs=[anywhere] * 3,
        out_shape=[jax.ShapeDtypeStruct(own.shape, own.dtype)] * 3,
        scratch_shapes=[
            pltpu.SemaphoreType.DMA((2 * GATHER_CHUNKS + 1,)),
            pltpu.SemaphoreType.DMA((2 * GATHER_CHUNKS + 1,)),
        ],
        compiler_params=pltpu.CompilerParams(collective_id=0, has_side_effects=True),
    )(own)


def upper_blocks(width):
    blocks = width // BLOCK
    return [(i, k) for i in range(blocks) for k in range(i, blocks)]


def ordered(first, second, swap):
    left = jnp.where(swap, second, first)
    right = jnp.where(swap, first, second)
    return jnp.concatenate([left, right], axis=1)


def gram_kernel(offsets, own, near, across, far, packed_ref, gram):
    step = pl.program_id(0)
    block_pairs = own.shape[0]
    rows_dev = pl.num_programs(0) * block_pairs * 2
    low, high, _ = slot_of(offsets, own_role(), lax.axis_index("bank") * rows_dev, rows_dev)
    start = step * block_pairs * 2
    feat = lax.axis_index("feat")
    swap = feat % 2 == 1
    parity = feat // 2

    @pl.when(step == 0)
    def _():
        gram[...] = jnp.zeros_like(gram)

    @pl.when(jnp.logical_and(start < high, start + 2 * block_pairs > low))
    def _():
        row = start + 2 * lax.broadcasted_iota(jnp.int32, (block_pairs, 1), 0)
        for first, second, shift in ((own, near, parity), (across, far, 1 - parity)):
            data = ordered(first[...], second[...], swap)
            keep = jnp.logical_and(row + shift >= low, row + shift < high)
            data = jnp.where(keep, data, jnp.zeros_like(data))
            gram[...] += lax.dot_general(
                data, data, (((0,), (0,)), ((), ())), preferred_element_type=jnp.float32
            )

    @pl.when(step == pl.num_programs(0) - 1)
    def _():
        for place, (i, k) in enumerate(upper_blocks(gram.shape[0])):
            packed_ref[place] = gram[i * BLOCK : (i + 1) * BLOCK, k * BLOCK : (k + 1) * BLOCK]


def own_gram(offsets, own, near, across, far):
    pair_rows, half = own.shape
    width = 2 * half
    block_pairs = min(256, pair_rows)
    packed = (len(upper_blocks(width)), BLOCK, BLOCK)
    return pl.pallas_call(
        gram_kernel,
        grid=(pair_rows // block_pairs,),
        in_specs=[pl.BlockSpec(memory_space=pltpu.SMEM)]
        + [pl.BlockSpec((block_pairs, half), lambda i: (i, 0))] * 4,
        out_specs=pl.BlockSpec(packed, lambda i: (0, 0, 0)),
        out_shape=jax.ShapeDtypeStruct(packed, jnp.float32),
        scratch_shapes=[pltpu.VMEM((width, width), jnp.float32)],
        compiler_params=pltpu.CompilerParams(vmem_limit_bytes=32 << 20),
    )(offsets, own, near, across, far)


def split_rows(value):
    high = value.astype(jnp.bfloat16).astype(jnp.float32)
    rest = value - high
    middle = rest.astype(jnp.bfloat16).astype(jnp.float32)
    low = (rest - middle).astype(jnp.bfloat16).astype(jnp.float32)
    return high, middle, low


def factor_block(work):
    for panel in range(BLOCK // SUB):
        base = panel * SUB
        rows = [work[base + i : base + i + 1, :] for i in range(SUB)]
        entry = {}
        for i in range(SUB):
            for k in range(i, SUB):
                column = base + k
                entry[i, k] = jnp.broadcast_to(rows[i][:, column : column + 1], (1, BLOCK))
        done = []
        for i in range(SUB):
            inverse_root = lax.rsqrt(entry[i, i])
            coefficient = {k: entry[i, k] * inverse_root for k in range(i + 1, SUB)}
            for k in range(i + 1, SUB):
                for m in range(k, SUB):
                    entry[k, m] = entry[k, m] - coefficient[k] * coefficient[m]
            scaled = rows[i] * jnp.concatenate([inverse_root, inverse_root], axis=1)
            done.append(scaled)
            for k in range(i + 1, SUB):
                both = jnp.concatenate([coefficient[k], coefficient[k]], axis=1)
                rows[k] = rows[k] - both * scaled
        for i in range(SUB):
            work[base + i : base + i + 1, :] = done[i]
        if base + SUB < BLOCK:
            high, middle, low = split_rows(work[base : base + SUB, :])
            left = jnp.concatenate([high, high, middle, high, middle, low], axis=0)
            right = jnp.concatenate([high, middle, high, low, middle, high], axis=0)
            update = lax.dot_general(
                left[:, :BLOCK].astype(jnp.bfloat16),
                right.astype(jnp.bfloat16),
                (((0,), (0,)), ((), ())),
                preferred_element_type=jnp.float32,
            )
            work[base + SUB :, :] = work[base + SUB :, :] - update[base + SUB :, :]


def whitener_kernel(rows_dev, offsets, own_ref, other_ref, out_ref, matrix, work):
    width = out_ref.shape[0]
    blocks = width // BLOCK
    role = own_role()
    row_start = lax.axis_index("bank") * rows_dev
    _, _, label = slot_of(offsets, role, row_start, rows_dev)
    left_open = jnp.logical_and(role == 0, offsets[label] < row_start)
    right_open = jnp.logical_and(role == TOUCH - 1, offsets[label + 1] > row_start + rows_dev)
    joined = jnp.logical_or(left_open, right_open)
    count = (offsets[label + 1] - offsets[label]).astype(jnp.float32)
    eye = (
        lax.broadcasted_iota(jnp.int32, (BLOCK, BLOCK), 0)
        == lax.broadcasted_iota(jnp.int32, (BLOCK, BLOCK), 1)
    ).astype(jnp.float32)
    for place, (i, k) in enumerate(upper_blocks(width)):
        total = own_ref[place] + jnp.where(joined, other_ref[place], 0.0)
        total = total / count
        if i == k:
            total = total + ridge_shift * eye
        else:
            matrix[k * BLOCK : (k + 1) * BLOCK, i * BLOCK : (i + 1) * BLOCK] = jnp.zeros_like(eye)
        matrix[i * BLOCK : (i + 1) * BLOCK, k * BLOCK : (k + 1) * BLOCK] = total

    @pl.loop(0, blocks)
    def _(j):
        here = pl.ds(pl.multiple_of(j * BLOCK, BLOCK), BLOCK)
        work[:, :BLOCK] = matrix[here, here]
        work[:, BLOCK:] = eye
        factor_block(work)
        matrix[here, here] = eye
        panel = lax.dot_general(
            work[:, BLOCK:],
            matrix[here, :],
            (((1,), (0,)), ((), ())),
            precision=lax.Precision.HIGHEST,
            preferred_element_type=jnp.float32,
        )
        matrix[here, :] = panel

        @pl.loop(j + 1, blocks)
        def _(i):
            there = pl.ds(pl.multiple_of(i * BLOCK, BLOCK), BLOCK)
            update = lax.dot_general(
                matrix[here, there],
                matrix[here, :],
                (((0,), (0,)), ((), ())),
                precision=lax.Precision.HIGHEST,
                preferred_element_type=jnp.float32,
            )
            matrix[there, here] = jnp.zeros_like(eye)
            matrix[there, :] = matrix[there, :] - update

        column = lax.broadcasted_iota(jnp.int32, (BLOCK, width), 1)
        final = jnp.where(column < (j + 1) * BLOCK, matrix[here, :], 0.0)
        out_ref[here, :] = final.astype(jnp.bfloat16)


def own_whitener(rows_dev, width, offsets, own, other):
    return pl.pallas_call(
        functools.partial(whitener_kernel, rows_dev),
        in_specs=[
            pl.BlockSpec(memory_space=pltpu.SMEM),
            pl.BlockSpec(memory_space=pltpu.VMEM),
            pl.BlockSpec(memory_space=pltpu.VMEM),
        ],
        out_specs=pl.BlockSpec(memory_space=pltpu.VMEM),
        out_shape=jax.ShapeDtypeStruct((width, width), jnp.bfloat16),
        scratch_shapes=[
            pltpu.VMEM((width, width), jnp.float32),
            pltpu.VMEM((BLOCK, 2 * BLOCK), jnp.float32),
        ],
        compiler_params=pltpu.CompilerParams(vmem_limit_bytes=32 << 20),
    )(offsets, own, other)


def spread_kernel(whitener, rows_ref, send, receive, local):
    bank, sibling, partner, diagonal = neighbours()
    feat = lax.axis_index("feat")
    half = rows_ref.shape[1]
    strips = half // BLOCK
    greet(bank, (sibling, partner, diagonal))

    def copies(place, device, upper):
        made = []
        for i in range(strips):
            first = (0 if upper else half) + i * BLOCK
            columns = pl.ds(0, first + BLOCK)
            made.append(
                pltpu.make_async_remote_copy(
                    src_ref=whitener.at[pl.ds(first, BLOCK), columns],
                    dst_ref=rows_ref.at[feat, pl.ds(i * BLOCK, BLOCK), columns],
                    send_sem=send.at[place, i],
                    recv_sem=receive.at[place, i],
                    device_id=(bank, device),
                    device_id_type=MESH,
                )
            )
        return made

    for upper_mine in (True, False):

        @pl.when(feat % 2 == (0 if upper_mine else 1))
        def _():
            sent = (
                copies(0, partner, upper_mine)
                + copies(1, diagonal, not upper_mine)
                + copies(2, sibling, not upper_mine)
            )
            for copy in sent:
                copy.start()
            source = whitener.at[pl.ds(0 if upper_mine else half, half), :]
            stay = pltpu.make_async_copy(source, rows_ref.at[feat], local)
            stay.start()
            for copy in sent:
                copy.wait_send()
            stay.wait()
            got = (
                copies(0, partner, upper_mine)
                + copies(1, diagonal, upper_mine)
                + copies(2, sibling, upper_mine)
            )
            for copy in got:
                copy.wait_recv()


def spread(whitener):
    width = whitener.shape[0]
    half = width // 2
    anywhere = pl.BlockSpec(memory_space=pl.ANY)
    return pl.pallas_call(
        spread_kernel,
        in_specs=[anywhere],
        out_specs=anywhere,
        out_shape=jax.ShapeDtypeStruct((TOUCH, half, width), whitener.dtype),
        scratch_shapes=[
            pltpu.SemaphoreType.DMA((3, half // BLOCK)),
            pltpu.SemaphoreType.DMA((3, half // BLOCK)),
            pltpu.SemaphoreType.DMA,
        ],
        compiler_params=pltpu.CompilerParams(collective_id=1, has_side_effects=True),
    )(whitener)


def whiten_kernel(offsets, own, near, factor_ref, out_ref, factors, total):
    step = pl.program_id(0)
    block_pairs, half = own.shape
    rows_dev = pl.num_programs(0) * block_pairs * 2
    bank, feat = lax.axis_index("bank"), lax.axis_index("feat")
    start = step * block_pairs * 2

    @pl.when(step == 0)
    def _():
        shape = factor_ref.shape[1:]
        row = (feat % 2) * half + lax.broadcasted_iota(jnp.int32, shape, 0)
        inside = lax.broadcasted_iota(jnp.int32, shape, 1) <= row
        for place in range(TOUCH):
            rows = factor_ref[place]
            factors[place] = jnp.where(inside, rows, jnp.zeros_like(rows))

    total[...] = jnp.zeros_like(total)
    for role in range(TOUCH):
        low, high, _ = slot_of(offsets, jnp.int32(role), bank * rows_dev, rows_dev)

        @pl.when(jnp.logical_and(start < high, start + 2 * block_pairs > low))
        def _():
            place = jnp.where(bank % 2 == 0, role, TOUCH - 1 - role)
            row = start + feat // 2 + 2 * lax.broadcasted_iota(jnp.int32, (block_pairs, 1), 0)
            data = ordered(own[...], near[...], feat % 2 == 1)
            keep = jnp.logical_and(row >= low, row < high)
            data = jnp.where(keep, data, jnp.zeros_like(data))
            total[...] += lax.dot_general(
                data, factors[place], (((1,), (1,)), ((), ())), preferred_element_type=jnp.float32
            )

    out_ref[...] = total[...].astype(jnp.bfloat16)


def whiten(offsets, own, near, factor_rows):
    pair_rows, half = own.shape
    block_pairs = min(256, pair_rows)
    block = pl.BlockSpec((block_pairs, half), lambda i: (i, 0))
    return pl.pallas_call(
        whiten_kernel,
        grid=(pair_rows // block_pairs,),
        in_specs=[
            pl.BlockSpec(memory_space=pltpu.SMEM),
            block,
            block,
            pl.BlockSpec(factor_rows.shape, lambda i: (0, 0, 0)),
        ],
        out_specs=block,
        out_shape=jax.ShapeDtypeStruct((pair_rows, half), jnp.bfloat16),
        scratch_shapes=[
            pltpu.VMEM(factor_rows.shape, jnp.bfloat16),
            pltpu.VMEM((block_pairs, half), jnp.float32),
        ],
        compiler_params=pltpu.CompilerParams(vmem_limit_bytes=32 << 20),
    )(offsets, own, near, factor_rows)


def meeting_pairs(bank_count, feat_count):
    pairs = []
    for bank in range(bank_count - 1):
        place = feat_count - 1 if bank % 2 == 0 else 0
        left, right = bank * feat_count + place, (bank + 1) * feat_count + place
        pairs += [(left, right), (right, left)]
    return pairs


def shards(bank_rows, offsets):
    pair_rows, out_width = bank_rows.shape
    near, across, far = gather_rows(bank_rows)
    own = own_gram(offsets, bank_rows, near, across, far)
    pairs = meeting_pairs(lax.axis_size("bank"), lax.axis_size("feat"))
    other = lax.ppermute(own, ("bank", "feat"), pairs)
    inverse = own_whitener(pair_rows * 2, 2 * out_width, offsets, own, other)
    return whiten(offsets, bank_rows, near, spread(inverse))


def solution(mesh):
    return jax.shard_map(
        shards,
        mesh=mesh,
        in_specs=(P("bank", "feat"), P()),
        out_specs=P("bank", "feat"),
        check_vma=False,
    )
```

time: 187 us -> 135 us (0.72)
  waiting for transfers between devices: 81.1 us -> 18.7 us
  Pallas kernels: 59.3 us -> 107 us
  between operations: 17.7 us -> 0.09 us
  other arithmetic: 7.67 us -> 0 us
  starting transfers between devices: 9.53 us -> 2.43 us
  local copies, waits for them, and re-layouts: 9.76 us -> 6.48 us
    pallas_call x3 -> x5, Pallas kernels: 59.3 us -> 107 us  [the longest x1 44.5 us: own_whitener(): pl.pallas_call(functools.partial(whitener_kernel, rows_dev), in_specs=[pl...]
    all_gather x1 -> x0, waiting for transfers between devices: 31.2 us -> none  [shards(): pairs = lax.all_gather(bank_rows, 'feat', axis=1, tiled=True)]
    all_to_all x1 -> x0, waiting for transfers between devices: 28.4 us -> none  [shards(): lax.all_to_all(outgoing, 'feat', split_axis=0, concat_axis=0, tiled=True)]
    all_to_all x1 -> x0, starting transfers between devices: 3.63 us -> none  [shards(): lax.all_to_all(outgoing, 'feat', split_axis=0, concat_axis=0, tiled=True)]
    ppermute x1, starting transfers between devices: 5.89 us -> 2.43 us  [shards(): other = lax.ppermute(own, ('bank', 'feat'), pairs)]
    gather x2 -> x0, local copies, waits for them, and re-layouts: 2.59 us -> none  [the longest x1 1.3 us: slot_bounds(): low = jnp.clip(offsets[labels] - row_start, 0, rows_dev)]
    dynamic_slice x4 -> x0, local copies, waits for them, and re-layouts: 2.5 us -> none  [the longest x2 1.32 us: shards(): own = own_gram(pairs, jnp.stack([low[role], high[role]]))]
    ppermute x1, waiting for transfers between devices: 20.8 us -> 18.7 us  [shards(): other = lax.ppermute(own, ('bank', 'feat'), pairs)]
  transfers between devices with their start and end apart: 3 -> 1, of which waited for: 3 -> 1; matrix products, arithmetic and copies ran while one was open for 6% -> 0% of each run, Pallas kernels for 0% -> 0%
where the time goes in v2:
time: 135 us; the launch traced here: 134 us
  Pallas kernels  107 us (79%)
  waiting for transfers between devices  18.7 us (14%)
  local copies, waits for them, and re-layouts  6.48 us (5%)
  starting transfers between devices  2.43 us (2%)
    pallas_call x1, Pallas kernels, own_whitener(): pl.pallas_call(functools.partial(whitener_kernel, rows_dev), in_specs=[pl...  44.5 us
    pallas_call x1, Pallas kernels, gather_rows(): pl.pallas_call(gather_kernel, in_specs=[anywhere], out_specs=[anywhere] *...  30.2 us
    pallas_call x1, Pallas kernels, spread(): pl.pallas_call(spread_kernel, in_specs=[anywhere], out_specs=anywhere, ou...  19.2 us
    ppermute x1, waiting for transfers between devices, shards(): other = lax.ppermute(own, ('bank', 'feat'), pairs)  18.7 us
    pallas_call x1, Pallas kernels, whiten(): pl.pallas_call(whiten_kernel, grid=(pair_rows // block_pairs,), in_specs=...  8.52 us
    unnamed x16, local copies, waits for them, and re-layouts  6.48 us
    pallas_call x1, Pallas kernels, own_gram(): pl.pallas_call(gram_kernel, grid=(pair_rows // block_pairs,), in_specs=[p...  4.43 us
  transfers between devices with their start and end apart: 1, of which 1 were waited for; matrix products, arithmetic and copies ran while one was open for 0% of the time, Pallas kernels for 0%

profile of v2, /device:TPU:8, one launch (start us, length us, event | category | flops | bytes accessed | tf_op | source)
XLA Modules:
  0.0 134.4 jit_solution(18212624802573600314)
XLA Ops:
  0.0 0.0 copy-start
  0.0 0.0 copy-start.7
  0.0 30.2 %shard_map.28 = (bf16[1536,384]{1,0:T(8,128)(2,1)}, bf16[1536,384]{1,0:T(8,128)(2,1)}, bf16[1536,384]{1,0:T(8,128)(2,1)}) custom-call(bf16[1536,384]{1,0:T(8,128)(2,1)} %own.5), custom_call_target="tpu_custom_call" | custom-call | tf_op jit(solution)/shard_map/pallas_call | solution.py:95
  30.2 0.0 copy-done
  30.2 0.0 copy-done.7
  30.2 0.0 copy-start.3
  30.2 1.3 copy-done.3
  31.5 0.0 copy-start.5
  31.5 1.3 copy-done.5
  32.7 0.0 copy-start.6
  32.7 1.3 copy-done.6
  34.0 4.4 %shard_map.29.own_ref = f32[21,128,128]{2,1,0:T(8,128)S(1)} custom-call(s32[17]{0:T(128)S(1)} %copy-done.7, bf16[1536,384]{1,0:T(8,128)(2,1)S(1)} %copy-done, bf16[1536,384]{1,0:T(8,128)(2,1)S(1)} %copy-done.3, bf16[1536,384]{1,0:T(8,128)(2,1)S(1)} %copy-done.5, bf16[1536,384]{1,0:T(8,128)(2,1)S(1)} %copy-done.6), custom_call_target="tpu_custom_call" | custom-call | tf_op jit(solution)/shard_map/pallas_call | solution.py:155
  38.4 2.4 %collective-permute-start = (f32[21,128,128]{2,1,0:T(8,128)S(1)}, f32[21,128,128]{2,1,0:T(8,128)S(1)}, u32[]{:S(2)}, u32[]{:S(2)}) collective-permute-start(f32[21,128,128]{2,1,0:T(8,128)S(1)} %shard_map.29.own_ref), channel_id=1, source_target_pairs={{3,7},{7,3},{4,8},{8,4},{11,15},{15,11},{12,16},{16,12},{19,23},{2... | collective-permute-start | bytes 4128776 | tf_op jit(solution)/shard_map/ppermute | solution.py:425
  40.9 18.7 %collective-permute-done.other_ref = f32[21,128,128]{2,1,0:T(8,128)S(1)} collective-permute-done((f32[21,128,128]{2,1,0:T(8,128)S(1)}, f32[21,128,128]{2,1,0:T(8,128)S(1)}, u32[]{:S(2)}, u32[]{:S(2)}) %collective-permute-start) | collective-permute-done | bytes 1376288 | tf_op jit(solution)/shard_map/ppermute | solution.py:425
  59.6 44.5 %shard_map.30.whitener = bf16[768,768]{1,0:T(8,128)(2,1)S(1)} custom-call(s32[17]{0:T(128)S(1)} %copy-done.7, f32[21,128,128]{2,1,0:T(8,128)S(1)} %shard_map.29.own_ref, f32[21,128,128]{2,1,0:T(8,128)S(1)} %collective-permute-done.other_ref), custom_call_target="tpu_custom_call" | custom-call | tf_op jit(solution)/shard_map/pallas_call | solution.py:269
  104.0 0.0 copy-start.2
  104.0 1.0 copy-done.2
  105.0 0.0 copy-start.4
  105.1 19.2 %shard_map.31.factor_ref = bf16[4,384,768]{2,1,0:T(8,128)(2,1)} custom-call(bf16[768,768]{1,0:T(8,128)(2,1)} %copy-done.2), custom_call_target="tpu_custom_call" | custom-call | tf_op jit(solution)/shard_map/pallas_call | solution.py:340
  124.2 0.0 copy-done.4
  124.3 0.0 copy-start.1
  124.3 1.7 %copy-done.1 = bf16[4,384,768]{2,1,0:T(8,128)(2,1)S(1)} copy-done((bf16[4,384,768]{2,1,0:T(8,128)(2,1)S(1)}, bf16[4,384,768]{2,1,0:T(8,128)(2,1)}, u32[]{:S(2)}) %copy-start.1) | copy-done | bytes 2359320
  125.9 8.5 %shard_map.32 = bf16[1536,384]{1,0:T(8,128)(2,1)} custom-call(s32[17]{0:T(128)S(1)} %copy-done.7, bf16[1536,384]{1,0:T(8,128)(2,1)S(1)} %copy-done, bf16[1536,384]{1,0:T(8,128)(2,1)S(1)} %copy-done.4, bf16[4,384,768]{2,1,0:T(8,128)(2,1)S(1)} %copy-done.1), custom_call_target="tpu_custom_call" | custom-call | tf_op jit(solution)/shard_map/pallas_call | solution.py:392
Async XLA Ops:
  0.0 30.2 %copy-start = (bf16[1536,384]{1,0:T(8,128)(2,1)S(1)}, bf16[1536,384]{1,0:T(8,128)(2,1)}, u32[]{:S(2)}) copy-start(bf16[1536,384]{1,0:T(8,128)(2,1)} %own.5) | copy-start | bytes 3538948
  0.0 30.2 %copy-start.7 = (s32[17]{0:T(128)S(1)}, s32[17]{0:T(128)}, u32[]{:S(2)}) copy-start(s32[17]{0:T(128)} %offsets.5) | copy-start | bytes 208
  30.2 1.3 copy-start.3
  31.5 1.3 copy-start.5
  32.7 1.3 copy-start.6
  38.4 21.1 %collective-permute-start = (f32[21,128,128]{2,1,0:T(8,128)S(1)}, f32[21,128,128]{2,1,0:T(8,128)S(1)}, u32[]{:S(2)}, u32[]{:S(2)}) collective-permute-start(f32[21,128,128]{2,1,0:T(8,128)S(1)} %shard_map.29.own_ref), channel_id=1, source_target_pairs={{3,7},{7,3},{4,8},{8,4},{11,15},{15,11},{12,16},{16,12},{19,23},{2... | collective-permute-start | bytes 4128776 | tf_op jit(solution)/shard_map/ppermute | solution.py:425
  104.0 1.0 copy-start.2
  105.0 19.2 %copy-start.4 = (bf16[1536,384]{1,0:T(8,128)(2,1)S(1)}, bf16[1536,384]{1,0:T(8,128)(2,1)}, u32[]{:S(2)}) copy-start(bf16[1536,384]{1,0:T(8,128)(2,1)} %get-tuple-element.8.near) | copy-start | bytes 3538948
  124.3 1.7 %copy-start.1 = (bf16[4,384,768]{2,1,0:T(8,128)(2,1)S(1)}, bf16[4,384,768]{2,1,0:T(8,128)(2,1)}, u32[]{:S(2)}) copy-start(bf16[4,384,768]{2,1,0:T(8,128)(2,1)} %shard_map.31.factor_ref) | copy-start | bytes 7077892

commit v3 on v2

--- a/solution.py
+++ b/solution.py
@@ -208,11 +208,51 @@
             work[base + SUB :, :] = work[base + SUB :, :] - update[base + SUB :, :]
 
 
-def whitener_kernel(rows_dev, offsets, own_ref, other_ref, out_ref, matrix, work):
-    width = out_ref.shape[0]
+def whitener_kernel(
+    rows_dev, bank_count, offsets, own_ref, rows_ref, other, matrix, work, final,
+    swap_send, swap_receive, send, receive, local,
+):
+    width = matrix.shape[0]
+    half = width // 2
     blocks = width // BLOCK
+    strips = half // BLOCK
+    bank, sibling, partner, diagonal = neighbours()
+    feat = lax.axis_index("feat")
     role = own_role()
-    row_start = lax.axis_index("bank") * rows_dev
+    meets_left = jnp.logical_and(role == 0, bank > 0)
+    meets_right = jnp.logical_and(role == TOUCH - 1, bank < bank_count - 1)
+    meets = jnp.logical_or(meets_left, meets_right)
+    met = jnp.where(meets_left, bank - 1, bank + 1)
+
+    barrier = pltpu.get_barrier_semaphore()
+    for device in (sibling, partner, diagonal):
+        pl.semaphore_signal(barrier, inc=1, device_id=(bank, device), device_id_type=MESH)
+
+    def swap(i):
+        place = sum(blocks - k for k in range(i))
+        span = pl.ds(place, blocks - i)
+        return pltpu.make_async_remote_copy(
+            src_ref=own_ref.at[span],
+            dst_ref=other.at[span],
+            send_sem=swap_send.at[i],
+            recv_sem=swap_receive.at[i],
+            device_id=(met, feat),
+            device_id_type=MESH,
+        )
+
+    @pl.when(meets)
+    def _():
+        pl.semaphore_signal(barrier, inc=1, device_id=(met, feat), device_id_type=MESH)
+        pl.semaphore_wait(barrier, 4)
+        for i in range(blocks):
+            swap(i).start()
+
+    @pl.when(jnp.logical_not(meets))
+    def _():
+        pl.semaphore_wait(barrier, 3)
+        other[...] = jnp.zeros_like(other)
+
+    row_start = bank * rows_dev
     _, _, label = slot_of(offsets, role, row_start, rows_dev)
     left_open = jnp.logical_and(role == 0, offsets[label] < row_start)
     right_open = jnp.logical_and(role == TOUCH - 1, offsets[label + 1] > row_start + rows_dev)
@@ -222,18 +262,58 @@
         lax.broadcasted_iota(jnp.int32, (BLOCK, BLOCK), 0)
         == lax.broadcasted_iota(jnp.int32, (BLOCK, BLOCK), 1)
     ).astype(jnp.float32)
-    for place, (i, k) in enumerate(upper_blocks(width)):
-        total = own_ref[place] + jnp.where(joined, other_ref[place], 0.0)
-        total = total / count
-        if i == k:
-            total = total + ridge_shift * eye
-        else:
-            matrix[k * BLOCK : (k + 1) * BLOCK, i * BLOCK : (i + 1) * BLOCK] = jnp.zeros_like(eye)
-        matrix[i * BLOCK : (i + 1) * BLOCK, k * BLOCK : (k + 1) * BLOCK] = total
+
+    def strip(place, i, device):
+        columns = pl.ds(0, (i + 1) * BLOCK)
+        return pltpu.make_async_remote_copy(
+            src_ref=final.at[pl.ds(i * BLOCK, BLOCK), columns],
+            dst_ref=rows_ref.at[feat, pl.ds(i % strips * BLOCK, BLOCK), columns],
+            send_sem=send.at[place, i % strips],
+            recv_sem=receive.at[place, i % strips],
+            device_id=(bank, device),
+            device_id_type=MESH,
+        )
+
+    def stay(i):
+        columns = pl.ds(0, (i + 1) * BLOCK)
+        return pltpu.make_async_copy(
+            final.at[pl.ds(i * BLOCK, BLOCK), columns],
+            rows_ref.at[feat, pl.ds(i % strips * BLOCK, BLOCK), columns],
+            local.at[i % strips],
+        )
 
     @pl.loop(0, blocks)
     def _(j):
         here = pl.ds(pl.multiple_of(j * BLOCK, BLOCK), BLOCK)
+        for i in range(blocks):
+
+            @pl.when(j == i)
+            def _():
+                @pl.when(meets)
+                def _():
+                    swap(i).wait_recv()
+
+                for k in range(i, blocks):
+                    place = sum(blocks - n for n in range(i)) + k - i
+                    total = own_ref[place] + jnp.where(joined, other[place], 0.0)
+                    total = total / count
+                    if i == k:
+                        total = total + ridge_shift * eye
+                    matrix[i * BLOCK : (i + 1) * BLOCK, k * BLOCK : (k + 1) * BLOCK] = total
+
+        @pl.loop(0, j)
+        def _(k):
+            above = pl.ds(pl.multiple_of(k * BLOCK, BLOCK), BLOCK)
+            update = lax.dot_general(
+                matrix[above, here],
+                matrix[above, :],
+                (((0,), (0,)), ((), ())),
+                precision=lax.Precision.HIGHEST,
+                preferred_element_type=jnp.float32,
+            )
+            matrix[here, above] = jnp.zeros_like(eye)
+            matrix[here, :] = matrix[here, :] - update
+
         work[:, :BLOCK] = matrix[here, here]
         work[:, BLOCK:] = eye
         factor_block(work)
@@ -246,109 +326,68 @@
             preferred_element_type=jnp.float32,
         )
         matrix[here, :] = panel
-
-        @pl.loop(j + 1, blocks)
-        def _(i):
-            there = pl.ds(pl.multiple_of(i * BLOCK, BLOCK), BLOCK)
-            update = lax.dot_general(
-                matrix[here, there],
-                matrix[here, :],
-                (((0,), (0,)), ((), ())),
-                precision=lax.Precision.HIGHEST,
-                preferred_element_type=jnp.float32,
-            )
-            matrix[there, here] = jnp.zeros_like(eye)
-            matrix[there, :] = matrix[there, :] - update
-
-        column = lax.broadcasted_iota(jnp.int32, (BLOCK, width), 1)
-        final = jnp.where(column < (j + 1) * BLOCK, matrix[here, :], 0.0)
-        out_ref[here, :] = final.astype(jnp.bfloat16)
-
-
-def own_whitener(rows_dev, width, offsets, own, other):
+        final[here, :] = panel.astype(jnp.bfloat16)
+        for i in range(blocks):
+            mine = 0 if i < strips else 1
+
+            @pl.when(jnp.logical_and(j == i, feat % 2 == mine))
+            def _():
+                strip(0, i, partner).start()
+                stay(i).start()
+
+            @pl.when(jnp.logical_and(j == i, feat % 2 != mine))
+            def _():
+                strip(1, i, diagonal).start()
+                strip(2, i, sibling).start()
+
+    @pl.when(meets)
+    def _():
+        for i in range(blocks):
+            swap(i).wait_send()
+
+    for parity in range(2):
+
+        @pl.when(feat % 2 == parity)
+        def _():
+            for i in range(strips):
+                mine, others = parity * strips + i, (1 - parity) * strips + i
+                strip(0, mine, partner).wait_send()
+                strip(1, others, diagonal).wait_send()
+                strip(2, others, sibling).wait_send()
+                stay(mine).wait()
+            for i in range(strips):
+                mine = parity * strips + i
+                strip(0, mine, partner).wait_recv()
+                strip(1, mine, diagonal).wait_recv()
+                strip(2, mine, sibling).wait_recv()
+
+
+def whitener_rows(rows_dev, width, offsets, own):
+    half, blocks = width // 2, width // BLOCK
+    strips = half // BLOCK
     return pl.pallas_call(
-        functools.partial(whitener_kernel, rows_dev),
+        functools.partial(whitener_kernel, rows_dev, lax.axis_size("bank")),
         in_specs=[
             pl.BlockSpec(memory_space=pltpu.SMEM),
             pl.BlockSpec(memory_space=pltpu.VMEM),
-            pl.BlockSpec(memory_space=pltpu.VMEM),
         ],
-        out_specs=pl.BlockSpec(memory_space=pltpu.VMEM),
-        out_shape=jax.ShapeDtypeStruct((width, width), jnp.bfloat16),
+        out_specs=pl.BlockSpec(memory_space=pl.ANY),
+        out_shape=jax.ShapeDtypeStruct((TOUCH, half, width), jnp.bfloat16),
         scratch_shapes=[
+            pltpu.VMEM(own.shape, jnp.float32),
             pltpu.VMEM((width, width), jnp.float32),
             pltpu.VMEM((BLOCK, 2 * BLOCK), jnp.float32),
+            pltpu.VMEM((width, width), jnp.bfloat16),
+            pltpu.SemaphoreType.DMA((blocks,)),
+            pltpu.SemaphoreType.DMA((blocks,)),
+            pltpu.SemaphoreType.DMA((3, strips)),
+            pltpu.SemaphoreType.DMA((3, strips)),
+            pltpu.SemaphoreType.DMA((strips,)),
         ],
-        compiler_params=pltpu.CompilerParams(vmem_limit_bytes=32 << 20),
-    )(offsets, own, other)
-
-
-def spread_kernel(whitener, rows_ref, send, receive, local):
-    bank, sibling, partner, diagonal = neighbours()
-    feat = lax.axis_index("feat")
-    half = rows_ref.shape[1]
-    strips = half // BLOCK
-    greet(bank, (sibling, partner, diagonal))
-
-    def copies(place, device, upper):
-        made = []
-        for i in range(strips):
-            first = (0 if upper else half) + i * BLOCK
-            columns = pl.ds(0, first + BLOCK)
-            made.append(
-                pltpu.make_async_remote_copy(
-                    src_ref=whitener.at[pl.ds(first, BLOCK), columns],
-                    dst_ref=rows_ref.at[feat, pl.ds(i * BLOCK, BLOCK), columns],
-                    send_sem=send.at[place, i],
-                    recv_sem=receive.at[place, i],
-                    device_id=(bank, device),
-                    device_id_type=MESH,
-                )
-            )
-        return made
-
-    for upper_mine in (True, False):
-
-        @pl.when(feat % 2 == (0 if upper_mine else 1))
-        def _():
-            sent = (
-                copies(0, partner, upper_mine)
-                + copies(1, diagonal, not upper_mine)
-                + copies(2, sibling, not upper_mine)
-            )
-            for copy in sent:
-                copy.start()
-            source = whitener.at[pl.ds(0 if upper_mine else half, half), :]
-            stay = pltpu.make_async_copy(source, rows_ref.at[feat], local)
-            stay.start()
-            for copy in sent:
-                copy.wait_send()
-            stay.wait()
-            got = (
-                copies(0, partner, upper_mine)
-                + copies(1, diagonal, upper_mine)
-                + copies(2, sibling, upper_mine)
-            )
-            for copy in got:
-                copy.wait_recv()
-
-
-def spread(whitener):
-    width = whitener.shape[0]
-    half = width // 2
-    anywhere = pl.BlockSpec(memory_space=pl.ANY)
-    return pl.pallas_call(
-        spread_kernel,
-        in_specs=[anywhere],
-        out_specs=anywhere,
-        out_shape=jax.ShapeDtypeStruct((TOUCH, half, width), whitener.dtype),
-        scratch_shapes=[
-            pltpu.SemaphoreType.DMA((3, half // BLOCK)),
-            pltpu.SemaphoreType.DMA((3, half // BLOCK)),
-            pltpu.SemaphoreType.DMA,
-        ],
-        compiler_params=pltpu.CompilerParams(collective_id=1, has_side_effects=True),
-    )(whitener)
+        compiler_params=pltpu.CompilerParams(
+            collective_id=1, has_side_effects=True, vmem_limit_bytes=32 << 20
+        ),
+    )(offsets, own)
 
 
 def whiten_kernel(offsets, own, near, factor_ref, out_ref, factors, total):
@@ -408,23 +447,12 @@
     )(offsets, own, near, factor_rows)
 
 
-def meeting_pairs(bank_count, feat_count):
-    pairs = []
-    for bank in range(bank_count - 1):
-        place = feat_count - 1 if bank % 2 == 0 else 0
-        left, right = bank * feat_count + place, (bank + 1) * feat_count + place
-        pairs += [(left, right), (right, left)]
-    return pairs
-
-
 def shards(bank_rows, offsets):
     pair_rows, out_width = bank_rows.shape
     near, across, far = gather_rows(bank_rows)
     own = own_gram(offsets, bank_rows, near, across, far)
-    pairs = meeting_pairs(lax.axis_size("bank"), lax.axis_size("feat"))
-    other = lax.ppermute(own, ("bank", "feat"), pairs)
-    inverse = own_whitener(pair_rows * 2, 2 * out_width, offsets, own, other)
-    return whiten(offsets, bank_rows, near, spread(inverse))
+    factor_rows = whitener_rows(pair_rows * 2, 2 * out_width, offsets, own)
+    return whiten(offsets, bank_rows, near, factor_rows)
 
 
 def solution(mesh):

time: 135 us -> 106 us (0.79)
  waiting for transfers between devices: 18.7 us -> 0 us
  Pallas kernels: 107 us -> 101 us
  local copies, waits for them, and re-layouts: 6.48 us -> 3.82 us
  starting transfers between devices: 2.43 us -> 0 us
    ppermute x1 -> x0, waiting for transfers between devices: 18.7 us -> none  [shards(): other = lax.ppermute(own, ('bank', 'feat'), pairs)]
    pallas_call x2 -> x1, Pallas kernels: 63.7 us -> 59.9 us  [whitener_rows(): pl.pallas_call(functools.partial(whitener_kernel, rows_dev, lax.axis_size...]
    unnamed x16 -> x12, local copies, waits for them, and re-layouts: 6.48 us -> 3.82 us
    ppermute x1 -> x0, starting transfers between devices: 2.43 us -> none  [shards(): other = lax.ppermute(own, ('bank', 'feat'), pairs)]
    pallas_call x1, Pallas kernels: 4.43 us -> 2.69 us  [own_gram(): pl.pallas_call(gram_kernel, grid=(pair_rows // block_pairs,), in_specs=[p...]
  transfers between devices with their start and end apart: 1 -> 0, of which waited for: 1 -> 0; matrix products, arithmetic and copies ran while one was open for 0% -> 0% of each run, Pallas kernels for 0% -> 0%
where the time goes in v3:
time: 106 us; the launch traced here: 105 us
  Pallas kernels  101 us (95%)
  local copies, waits for them, and re-layouts  3.82 us (4%)
    pallas_call x1, Pallas kernels, whitener_rows(): pl.pallas_call(functools.partial(whitener_kernel, rows_dev, lax.axis_size...  59.9 us
    pallas_call x1, Pallas kernels, gather_rows(): pl.pallas_call(gather_kernel, in_specs=[anywhere], out_specs=[anywhere] *...  30.2 us
    pallas_call x1, Pallas kernels, whiten(): pl.pallas_call(whiten_kernel, grid=(pair_rows // block_pairs,), in_specs=...  8.56 us
    unnamed x12, local copies, waits for them, and re-layouts  3.82 us
    pallas_call x1, Pallas kernels, own_gram(): pl.pallas_call(gram_kernel, grid=(pair_rows // block_pairs,), in_specs=[p...  2.69 us

profile of v3, /device:TPU:8, one launch (start us, length us, event | category | flops | bytes accessed | tf_op | source)
XLA Modules:
  0.0 105.2 jit_solution(9030054626894926096)
XLA Ops:
  0.0 0.0 copy-start.5
  0.0 0.0 copy-start
  0.0 30.2 %shard_map.28 = (bf16[1536,384]{1,0:T(8,128)(2,1)}, bf16[1536,384]{1,0:T(8,128)(2,1)}, bf16[1536,384]{1,0:T(8,128)(2,1)}) custom-call(bf16[1536,384]{1,0:T(8,128)(2,1)} %own.5), custom_call_target="tpu_custom_call" | custom-call | tf_op jit(solution)/shard_map/pallas_call | solution.py:95
  30.2 0.0 copy-done.5
  30.2 0.0 copy-done
  30.2 0.0 copy-start.1
  30.2 1.3 %copy-done.1 = bf16[1536,384]{1,0:T(8,128)(2,1)S(1)} copy-done((bf16[1536,384]{1,0:T(8,128)(2,1)S(1)}, bf16[1536,384]{1,0:T(8,128)(2,1)}, u32[]{:S(2)}) %copy-start.1) | copy-done | bytes 1179672
  31.5 0.0 copy-start.3
  31.5 1.3 %copy-done.3 = bf16[1536,384]{1,0:T(8,128)(2,1)S(1)} copy-done((bf16[1536,384]{1,0:T(8,128)(2,1)S(1)}, bf16[1536,384]{1,0:T(8,128)(2,1)}, u32[]{:S(2)}) %copy-start.3) | copy-done | bytes 1179672
  32.7 0.0 copy-start.4
  32.7 1.3 %copy-done.4 = bf16[1536,384]{1,0:T(8,128)(2,1)S(1)} copy-done((bf16[1536,384]{1,0:T(8,128)(2,1)S(1)}, bf16[1536,384]{1,0:T(8,128)(2,1)}, u32[]{:S(2)}) %copy-start.4) | copy-done | bytes 1179672
  34.0 2.7 %shard_map.29.own_ref = f32[21,128,128]{2,1,0:T(8,128)S(1)} custom-call(s32[17]{0:T(128)S(1)} %copy-done.5, bf16[1536,384]{1,0:T(8,128)(2,1)S(1)} %copy-done, bf16[1536,384]{1,0:T(8,128)(2,1)S(1)} %copy-done.1, bf16[1536,384]{1,0:T(8,128)(2,1)S(1)} %copy-done.3, bf16[1536,384]{1,0:T(8,128)(2,1)S(1)} %copy-done.4), custom_call_target="tpu_custom_call" | custom-call | tf_op jit(solution)/shard_map/pallas_call | solution.py:155
  36.7 0.0 copy-start.2
  36.7 59.9 %shard_map.30.factor_ref = bf16[4,384,768]{2,1,0:T(8,128)(2,1)S(1)} custom-call(s32[17]{0:T(128)S(1)} %copy-done.5, f32[21,128,128]{2,1,0:T(8,128)S(1)} %shard_map.29.own_ref), custom_call_target="tpu_custom_call" | custom-call | tf_op jit(solution)/shard_map/pallas_call | solution.py:368
  96.6 0.0 copy-done.2
  96.6 8.6 %shard_map.31 = bf16[1536,384]{1,0:T(8,128)(2,1)} custom-call(s32[17]{0:T(128)S(1)} %copy-done.5, bf16[1536,384]{1,0:T(8,128)(2,1)S(1)} %copy-done, bf16[1536,384]{1,0:T(8,128)(2,1)S(1)} %copy-done.2, bf16[4,384,768]{2,1,0:T(8,128)(2,1)S(1)} %shard_map.30.factor_ref), custom_call_target="tpu_custom_call" | custom-call | tf_op jit(solution)/shard_map/pallas_call | solution.py:431
Async XLA Ops:
  0.0 30.2 %copy-start.5 = (s32[17]{0:T(128)S(1)}, s32[17]{0:T(128)}, u32[]{:S(2)}) copy-start(s32[17]{0:T(128)} %offsets.5) | copy-start | bytes 208
  0.0 30.2 %copy-start = (bf16[1536,384]{1,0:T(8,128)(2,1)S(1)}, bf16[1536,384]{1,0:T(8,128)(2,1)}, u32[]{:S(2)}) copy-start(bf16[1536,384]{1,0:T(8,128)(2,1)} %own.5) | copy-start | bytes 3538948
  30.2 1.3 %copy-start.1 = (bf16[1536,384]{1,0:T(8,128)(2,1)S(1)}, bf16[1536,384]{1,0:T(8,128)(2,1)}, u32[]{:S(2)}) copy-start(bf16[1536,384]{1,0:T(8,128)(2,1)} %get-tuple-element.8.near) | copy-start | bytes 3538948
  31.5 1.3 %copy-start.3 = (bf16[1536,384]{1,0:T(8,128)(2,1)S(1)}, bf16[1536,384]{1,0:T(8,128)(2,1)}, u32[]{:S(2)}) copy-start(bf16[1536,384]{1,0:T(8,128)(2,1)} %get-tuple-element.9.across) | copy-start | bytes 3538948
  32.7 1.3 %copy-start.4 = (bf16[1536,384]{1,0:T(8,128)(2,1)S(1)}, bf16[1536,384]{1,0:T(8,128)(2,1)}, u32[]{:S(2)}) copy-start(bf16[1536,384]{1,0:T(8,128)(2,1)} %get-tuple-element.10.far) | copy-start | bytes 3538948
  36.7 59.9 %copy-start.2 = (bf16[1536,384]{1,0:T(8,128)(2,1)S(1)}, bf16[1536,384]{1,0:T(8,128)(2,1)}, u32[]{:S(2)}) copy-start(bf16[1536,384]{1,0:T(8,128)(2,1)} %get-tuple-element.8.near) | copy-start | bytes 3538948

commit v4 on v3

--- a/solution.py
+++ b/solution.py
@@ -14,7 +14,7 @@
 
 
 MESH = pl.DeviceIdType.MESH
-GATHER_CHUNKS = 4
+GATHER_CHUNKS = 6
 
 
 def slot_of(offsets, role, row_start, rows_dev):
@@ -54,10 +54,25 @@
     pl.semaphore_wait(barrier, len(others))
 
 
-def gather_kernel(own, near, across, far, send, receive):
+def upper_blocks(width):
+    blocks = width // BLOCK
+    return [(i, k) for i in range(blocks) for k in range(i, blocks)]
+
+
+def ordered(first, second, swap):
+    left = jnp.where(swap, second, first)
+    right = jnp.where(swap, first, second)
+    return jnp.concatenate([left, right], axis=1)
+
+
+def gram_kernel(
+    offsets, own, packed_ref, near_ref, kept, near, across, far, gram, send, receive, local
+):
     bank, sibling, partner, _ = neighbours()
     greet(bank, (sibling, partner))
-    piece = own.shape[0] // GATHER_CHUNKS
+    pair_rows, half = own.shape
+    piece = pair_rows // GATHER_CHUNKS
+    rows_dev = 2 * pair_rows
 
     def remote(source, target, place, device):
         return pltpu.make_async_remote_copy(
@@ -69,99 +84,94 @@
             device_id_type=MESH,
         )
 
-    firsts, seconds = [], []
-    for i in range(GATHER_CHUNKS):
-        span = pl.ds(i * piece, piece)
-        firsts.append(remote(own.at[span, :], across.at[span, :], i, partner))
-        seconds.append(
-            remote(across.at[span, :], far.at[span, :], GATHER_CHUNKS + i, sibling)
-        )
+    def part(i):
+        return pl.ds(pl.multiple_of(i * piece, piece), piece)
+
+    def crossing(i):
+        return remote(own.at[part(i), :], across.at[part(i), :], i, partner)
+
+    def passing(i):
+        return remote(across.at[part(i), :], far.at[part(i), :], GATHER_CHUNKS + i, sibling)
+
     beside = remote(own, near, 2 * GATHER_CHUNKS, sibling)
-    for copy in firsts:
-        copy.start()
+    fetch = pltpu.make_async_copy(own, kept, local.at[0])
+    keep_near = pltpu.make_async_copy(near, near_ref, local.at[1])
     beside.start()
-    for first, second in zip(firsts, seconds):
-        first.wait_recv()
-        second.start()
-    for copy in firsts:
-        copy.wait_send()
-    for copy in seconds:
-        copy.wait()
-    beside.wait()
-
-
-def gather_rows(own):
+
+    @pl.loop(0, GATHER_CHUNKS)
+    def _(i):
+        crossing(i).start()
+
+    fetch.start()
+    low, high, _ = slot_of(offsets, own_role(), bank * rows_dev, rows_dev)
+    feat = lax.axis_index("feat")
+    parity = feat // 2
+    gram[...] = jnp.zeros_like(gram)
+
+    def add(first, second, i, shift):
+        data = ordered(first[part(i), :], second[part(i), :], feat % 2 == 1)
+        row = 2 * (i * piece + lax.broadcasted_iota(jnp.int32, (piece, 1), 0)) + shift
+        inside = jnp.logical_and(row >= low, row < high)
+        data = jnp.where(inside, data, jnp.zeros_like(data))
+        gram[...] += lax.dot_general(
+            data, data, (((0,), (0,)), ((), ())), preferred_element_type=jnp.float32
+        )
+
+    fetch.wait()
+    beside.wait_recv()
+    keep_near.start()
+
+    @pl.loop(0, GATHER_CHUNKS)
+    def _(i):
+        add(kept, near, i, parity)
+
+    @pl.loop(0, GATHER_CHUNKS + 1)
+    def _(i):
+        @pl.when(i < GATHER_CHUNKS)
+        def _():
+            crossing(i).wait_recv()
+            passing(i).start()
+
+        @pl.when(i > 0)
+        def _():
+            passing(i - 1).wait_recv()
+            add(across, far, i - 1, 1 - parity)
+
+    for place, (i, k) in enumerate(upper_blocks(2 * half)):
+        packed_ref[place] = gram[i * BLOCK : (i + 1) * BLOCK, k * BLOCK : (k + 1) * BLOCK]
+
+    @pl.loop(0, GATHER_CHUNKS)
+    def _(i):
+        crossing(i).wait_send()
+        passing(i).wait_send()
+
+    beside.wait_send()
+    keep_near.wait()
+
+
+def own_gram(offsets, own):
+    width = 2 * own.shape[1]
+    packed = (len(upper_blocks(width)), BLOCK, BLOCK)
     anywhere = pl.BlockSpec(memory_space=pl.ANY)
     return pl.pallas_call(
-        gather_kernel,
-        in_specs=[anywhere],
-        out_specs=[anywhere] * 3,
-        out_shape=[jax.ShapeDtypeStruct(own.shape, own.dtype)] * 3,
-        scratch_shapes=[
+        gram_kernel,
+        in_specs=[pl.BlockSpec(memory_space=pltpu.SMEM), anywhere],
+        out_specs=[pl.BlockSpec(memory_space=pltpu.VMEM), anywhere],
+        out_shape=[
+            jax.ShapeDtypeStruct(packed, jnp.float32),
+            jax.ShapeDtypeStruct(own.shape, own.dtype),
+        ],
+        scratch_shapes=[pltpu.VMEM(own.shape, own.dtype)] * 4
+        + [
+            pltpu.VMEM((width, width), jnp.float32),
             pltpu.SemaphoreType.DMA((2 * GATHER_CHUNKS + 1,)),
             pltpu.SemaphoreType.DMA((2 * GATHER_CHUNKS + 1,)),
-        ],
-        compiler_params=pltpu.CompilerParams(collective_id=0, has_side_effects=True),
-    )(own)
-
-
-def upper_blocks(width):
-    blocks = width // BLOCK
-    return [(i, k) for i in range(blocks) for k in range(i, blocks)]
-
-
-def ordered(first, second, swap):
-    left = jnp.where(swap, second, first)
-    right = jnp.where(swap, first, second)
-    return jnp.concatenate([left, right], axis=1)
-
-
-def gram_kernel(offsets, own, near, across, far, packed_ref, gram):
-    step = pl.program_id(0)
-    block_pairs = own.shape[0]
-    rows_dev = pl.num_programs(0) * block_pairs * 2
-    low, high, _ = slot_of(offsets, own_role(), lax.axis_index("bank") * rows_dev, rows_dev)
-    start = step * block_pairs * 2
-    feat = lax.axis_index("feat")
-    swap = feat % 2 == 1
-    parity = feat // 2
-
-    @pl.when(step == 0)
-    def _():
-        gram[...] = jnp.zeros_like(gram)
-
-    @pl.when(jnp.logical_and(start < high, start + 2 * block_pairs > low))
-    def _():
-        row = start + 2 * lax.broadcasted_iota(jnp.int32, (block_pairs, 1), 0)
-        for first, second, shift in ((own, near, parity), (across, far, 1 - parity)):
-            data = ordered(first[...], second[...], swap)
-            keep = jnp.logical_and(row + shift >= low, row + shift < high)
-            data = jnp.where(keep, data, jnp.zeros_like(data))
-            gram[...] += lax.dot_general(
-                data, data, (((0,), (0,)), ((), ())), preferred_element_type=jnp.float32
-            )
-
-    @pl.when(step == pl.num_programs(0) - 1)
-    def _():
-        for place, (i, k) in enumerate(upper_blocks(gram.shape[0])):
-            packed_ref[place] = gram[i * BLOCK : (i + 1) * BLOCK, k * BLOCK : (k + 1) * BLOCK]
-
-
-def own_gram(offsets, own, near, across, far):
-    pair_rows, half = own.shape
-    width = 2 * half
-    block_pairs = min(256, pair_rows)
-    packed = (len(upper_blocks(width)), BLOCK, BLOCK)
-    return pl.pallas_call(
-        gram_kernel,
-        grid=(pair_rows // block_pairs,),
-        in_specs=[pl.BlockSpec(memory_space=pltpu.SMEM)]
-        + [pl.BlockSpec((block_pairs, half), lambda i: (i, 0))] * 4,
-        out_specs=pl.BlockSpec(packed, lambda i: (0, 0, 0)),
-        out_shape=jax.ShapeDtypeStruct(packed, jnp.float32),
-        scratch_shapes=[pltpu.VMEM((width, width), jnp.float32)],
-        compiler_params=pltpu.CompilerParams(vmem_limit_bytes=32 << 20),
-    )(offsets, own, near, across, far)
+            pltpu.SemaphoreType.DMA((2,)),
+        ],
+        compiler_params=pltpu.CompilerParams(
+            collective_id=0, has_side_effects=True, vmem_limit_bytes=32 << 20
+        ),
+    )(offsets, own)
 
 
 def split_rows(value):
@@ -390,7 +400,7 @@
     )(offsets, own)
 
 
-def whiten_kernel(offsets, own, near, factor_ref, out_ref, factors, total):
+def whiten_kernel(offsets, own, near, factor_ref, out_ref, factors, total, bounds):
     step = pl.program_id(0)
     block_pairs, half = own.shape
     rows_dev = pl.num_programs(0) * block_pairs * 2
@@ -402,13 +412,17 @@
         shape = factor_ref.shape[1:]
         row = (feat % 2) * half + lax.broadcasted_iota(jnp.int32, shape, 0)
         inside = lax.broadcasted_iota(jnp.int32, shape, 1) <= row
+        for role in range(TOUCH):
+            bounds[role], bounds[TOUCH + role], _ = slot_of(
+                offsets, jnp.int32(role), bank * rows_dev, rows_dev
+            )
         for place in range(TOUCH):
             rows = factor_ref[place]
             factors[place] = jnp.where(inside, rows, jnp.zeros_like(rows))
 
     total[...] = jnp.zeros_like(total)
     for role in range(TOUCH):
-        low, high, _ = slot_of(offsets, jnp.int32(role), bank * rows_dev, rows_dev)
+        low, high = bounds[role], bounds[TOUCH + role]
 
         @pl.when(jnp.logical_and(start < high, start + 2 * block_pairs > low))
         def _():
@@ -442,6 +456,7 @@
         scratch_shapes=[
             pltpu.VMEM(factor_rows.shape, jnp.bfloat16),
             pltpu.VMEM((block_pairs, half), jnp.float32),
+            pltpu.SMEM((2 * TOUCH,), jnp.int32),
         ],
         compiler_params=pltpu.CompilerParams(vmem_limit_bytes=32 << 20),
     )(offsets, own, near, factor_rows)
@@ -449,8 +464,7 @@
 
 def shards(bank_rows, offsets):
     pair_rows, out_width = bank_rows.shape
-    near, across, far = gather_rows(bank_rows)
-    own = own_gram(offsets, bank_rows, near, across, far)
+    own, near = own_gram(offsets, bank_rows)
     factor_rows = whitener_rows(pair_rows * 2, 2 * out_width, offsets, own)
     return whiten(offsets, bank_rows, near, factor_rows)
 

time: 106 us -> 97.1 us (0.916)
  Pallas kernels: 101 us -> 93.9 us
  local copies, waits for them, and re-layouts: 3.82 us -> 1.93 us
    pallas_call x1, Pallas kernels: 59.9 us -> 57 us  [whitener_rows(): pl.pallas_call(functools.partial(whitener_kernel, rows_dev, lax.axis_size...]
    pallas_call x2 -> x1, Pallas kernels: 32.9 us -> 30.2 us  [own_gram(): pl.pallas_call(gram_kernel, in_specs=[pl.BlockSpec(memory_space=pltpu.SME...]
    unnamed x12 -> x6, local copies, waits for them, and re-layouts: 3.82 us -> 1.93 us
    pallas_call x1, Pallas kernels: 8.56 us -> 6.7 us  [whiten(): pl.pallas_call(whiten_kernel, grid=(pair_rows // block_pairs,), in_specs=...]
where the time goes in v4:
time: 97.1 us; the launch traced here: 95.9 us
  Pallas kernels  93.9 us (97%)
  local copies, waits for them, and re-layouts  1.93 us (2%)
    pallas_call x1, Pallas kernels, whitener_rows(): pl.pallas_call(functools.partial(whitener_kernel, rows_dev, lax.axis_size...  57 us
    pallas_call x1, Pallas kernels, own_gram(): pl.pallas_call(gram_kernel, in_specs=[pl.BlockSpec(memory_space=pltpu.SME...  30.2 us
    pallas_call x1, Pallas kernels, whiten(): pl.pallas_call(whiten_kernel, grid=(pair_rows // block_pairs,), in_specs=...  6.7 us

profile of v4, /device:TPU:8, one launch (start us, length us, event | category | flops | bytes accessed | tf_op | source)
XLA Modules:
  0.0 95.9 jit_solution(4892514981803803385)
XLA Ops:
  0.0 0.0 copy-start
  0.0 1.3 %copy-done = bf16[1536,384]{1,0:T(8,128)(2,1)S(1)} copy-done((bf16[1536,384]{1,0:T(8,128)(2,1)S(1)}, bf16[1536,384]{1,0:T(8,128)(2,1)}, u32[]{:S(2)}) %copy-start) | copy-done | bytes 1179672
  1.3 0.0 copy-start.2
  1.3 0.7 copy-done.2
  1.9 30.2 %shard_map.28 = (f32[21,128,128]{2,1,0:T(8,128)S(1)}, bf16[1536,384]{1,0:T(8,128)(2,1)S(1)}) custom-call(s32[17]{0:T(128)S(1)} %copy-done.2, bf16[1536,384]{1,0:T(8,128)(2,1)S(1)} %copy-done), custom_call_target="tpu_custom_call" | custom-call | tf_op jit(solution)/shard_map/pallas_call | solution.py:156
  32.1 0.0 copy-start.1
  32.1 57.0 %shard_map.29.factor_ref = bf16[4,384,768]{2,1,0:T(8,128)(2,1)S(1)} custom-call(s32[17]{0:T(128)S(1)} %copy-done.2, f32[21,128,128]{2,1,0:T(8,128)S(1)} %get-tuple-element.8.own_ref), custom_call_target="tpu_custom_call" | custom-call | tf_op jit(solution)/shard_map/pallas_call | solution.py:378
  89.1 0.0 copy-done.1
  89.1 6.7 %shard_map.30 = bf16[1536,384]{1,0:T(8,128)(2,1)} custom-call(s32[17]{0:T(128)S(1)} %copy-done.2, bf16[1536,384]{1,0:T(8,128)(2,1)S(1)} %copy-done.1, bf16[1536,384]{1,0:T(8,128)(2,1)S(1)} %get-tuple-element.7.near, bf16[4,384,768]{2,1,0:T(8,128)(2,1)S(1)} %shard_map.29.factor_ref), custom_call_target="tpu_custom_call" | custom-call | tf_op jit(solution)/shard_map/pallas_call | solution.py:445
Async XLA Ops:
  0.0 1.3 %copy-start = (bf16[1536,384]{1,0:T(8,128)(2,1)S(1)}, bf16[1536,384]{1,0:T(8,128)(2,1)}, u32[]{:S(2)}) copy-start(bf16[1536,384]{1,0:T(8,128)(2,1)} %own.3) | copy-start | bytes 3538948
  1.3 0.7 copy-start.2
  32.1 57.0 %copy-start.1 = (bf16[1536,384]{1,0:T(8,128)(2,1)S(1)}, bf16[1536,384]{1,0:T(8,128)(2,1)}, u32[]{:S(2)}) copy-start(bf16[1536,384]{1,0:T(8,128)(2,1)} %own.3) | copy-start | bytes 3538948
